TPU v7x, 256 devices: a whole 4x4x8 slice. The times are simulated.
256 devices in a mesh: cells: 128 (over z, y, x_lo, core), lanes: 2 (over x_hi).
Axes of the slice: x: 4 (x_hi: 2, x_lo: 2; x = x_hi * 2 + x_lo), y: 4, z: 8, core: 2. Of those that a mesh axis runs over, the one named last changes fastest.
Arguments:
- centres: float32 [3, 131072], P(None, 'cells'), may hold values from 0 to 4
- seg_lines: float32 [3, 131072], P(None, 'cells'), may hold values from -3 to 3
- burgers: float32 [3, 131072], P(None, 'cells'), may hold values from -6 to 6
- neighbour_blocks: int32 [1024, 16], P('cells', 'lanes'), may hold values from 0 to 39
- seg_nodes: int32 [2, 131072], P(None, 'cells'), may hold values from 0 to 1023
- node_owner: int32 [2, 131072], P(None, 'cells'), may hold values from 0 to 1
- mobility: float32 [131072], P('cells'), may hold values from 0.5 to 4
- cand_target: int32 [4096], P('cells'), may hold values from 0 to 7
- cand_source: int32 [4096], P('cells'), may hold values from 0 to 39
Outputs:
- node_velocity: float32 [3, 131072], P(None, 'cells')
- nearness: float32 [131072], P('cells')
All inputs are finite; a program needn't handle non-finite values.
Results may differ from a plain program's by a relative error of at most 0.0003.
Values sent between devices are 32-bit elements; how exact they have to be, the bound alone decides.
A program may use at most 64 MiB of HBM per device.

v0:
```python
import jax
import jax.numpy as jnp
from jax import lax
from jax.sharding import PartitionSpec as P

BLK = 128
REACH = 2


FORCE_SCALE = 0.02
CORE_SQUARE = 0.25
TIME_STEP = 4.0
HIGH = lax.Precision.HIGHEST


def passed_along(block, axis, distance):
    devices = range(lax.axis_size(axis))
    route = [((i - distance) % len(devices), i) for i in devices]
    return lax.ppermute(block, axis, route)


def total_of_pieces(array, axis):
    parts = lax.all_gather(array, axis)
    return parts.sum(axis=0)


def cross_product(first, second):
    return jnp.stack(
        [
            first[1] * second[2] - first[2] * second[1],
            first[2] * second[0] - first[0] * second[2],
            first[0] * second[1] - first[1] * second[0],
        ]
    )


def tile_forces(own_blocks, source_blocks):
    target_centre = own_blocks[0:3]
    target_line = own_blocks[3:6]
    source_centre = source_blocks[0:3]
    source_line = source_blocks[3:6]
    source_burgers = source_blocks[6:9]
    along = jnp.einsum("ckj,cki->kij", source_burgers, target_line, precision=HIGH)
    separation = target_centre[:, :, :, None] - source_centre[:, :, None, :]
    square = jnp.sum(separation * separation, axis=0) + CORE_SQUARE
    inverse = lax.rsqrt(square)
    weight = along * inverse * inverse * inverse
    summed_line = jnp.einsum("kij,ckj->cki", weight, source_line, precision=HIGH)
    summed_moment = jnp.einsum(
        "kij,ckj->cki", weight, cross_product(source_line, source_centre), precision=HIGH
    )
    return FORCE_SCALE * (cross_product(summed_line, target_centre) - summed_moment)


def block_forces(own_blocks, window_blocks, block_lists):

    def add_entry(summed, column):
        chosen = jnp.take(window_blocks, column, axis=1)
        return (summed + tile_forces(own_blocks, chosen), None)

    initial = jnp.zeros((3,) + own_blocks.shape[1:], jnp.float32)
    summed, unused = lax.scan(add_entry, initial, jnp.transpose(block_lists))
    return summed


def swept_tiles(own_blocks, window_blocks, targets, sources):
    target_side = jnp.take(own_blocks, targets, axis=1)
    source_side = jnp.take(window_blocks, sources, axis=1)
    separation = target_side[0:3, :, :, None] - source_side[0:3, :, None, :]
    motion = TIME_STEP * (target_side[3:6, :, :, None] - source_side[3:6, :, None, :])
    approach = jnp.sum(separation * motion, axis=0)
    motion_square = jnp.sum(motion * motion, axis=0)
    fraction = jnp.clip(-approach / (motion_square + CORE_SQUARE), 0.0, 1.0)
    closest = separation + fraction[None] * motion
    distance = jnp.sum(closest * closest, axis=0)
    summed = jnp.sum(jnp.exp(-distance), axis=2)
    selector = (
        targets[:, None] == jnp.arange(own_blocks.shape[1], dtype=jnp.int32)[None, :]
    ).astype(jnp.float32)
    return jnp.einsum("nk,nb->kb", selector, summed, precision=HIGH)


def deposit(deposits, node_ids, keep_mask, node_count):
    masked = deposits * keep_mask.astype(jnp.float32)[None, :]
    return jnp.transpose(
        jax.ops.segment_sum(jnp.transpose(masked), node_ids, num_segments=node_count)
    )


def end_velocity(velocity, next_velocity, node_ids, owner_map):
    return jnp.where(
        owner_map[None, :] == 0,
        jnp.take(velocity, node_ids, axis=1),
        jnp.take(next_velocity, node_ids, axis=1),
    )


def local(
    centres,
    seg_lines,
    burgers,
    neighbour_blocks,
    seg_nodes,
    node_owner,
    mobility,
    cand_target,
    cand_source,
):
    seg_count = centres.shape[1]
    block_count = seg_count // BLK
    offsets = [shift_size for shift_size in range(-REACH, REACH + 1) if shift_size != 0]
    own_fields = jnp.concatenate([centres, seg_lines, burgers], 0)
    fetched = [passed_along(own_fields, "cells", -offset) for offset in offsets]
    window = jnp.concatenate(fetched[:REACH] + [own_fields] + fetched[REACH:], 1)
    own_blocks = own_fields.reshape(9, block_count, BLK)
    window_blocks = window.reshape(9, -1, BLK)
    partial_value = block_forces(own_blocks, window_blocks, neighbour_blocks).reshape(3, seg_count)
    forces = total_of_pieces(partial_value, "lanes")
    lengths = jnp.sqrt(jnp.sum(seg_lines * seg_lines, axis=0))
    deposits = jnp.concatenate([0.5 * forces, 0.5 * lengths[None, :]], 0)
    node_count = mobility.shape[0]
    own_part = deposit(deposits, seg_nodes[0], node_owner[0] == 0, node_count) + deposit(
        deposits, seg_nodes[1], node_owner[1] == 0, node_count
    )
    next_part = deposit(deposits, seg_nodes[0], node_owner[0] == 1, node_count) + deposit(
        deposits, seg_nodes[1], node_owner[1] == 1, node_count
    )
    received = passed_along(next_part, "cells", 1)
    totals = own_part + received
    velocity = mobility[None, :] * totals[0:3] / (1.0 + totals[3:4])
    next_velocity = passed_along(velocity, "cells", -1)
    seg_velocity = 0.5 * (
        end_velocity(velocity, next_velocity, seg_nodes[0], node_owner[0])
        + end_velocity(velocity, next_velocity, seg_nodes[1], node_owner[1])
    )
    moved = [passed_along(seg_velocity, "cells", -offset) for offset in offsets]
    window_velocity = jnp.concatenate(moved[:REACH] + [seg_velocity] + moved[REACH:], 1)
    window_motion = jnp.concatenate([window[0:3], window_velocity], 0).reshape(6, -1, BLK)
    own_motion = jnp.concatenate([centres, seg_velocity], 0).reshape(6, block_count, BLK)
    nearness = swept_tiles(own_motion, window_motion, cand_target, cand_source)
    return (velocity, nearness.reshape(seg_count))


def solution(mesh):
    in_specs = (
        P(None, "cells"),
        P(None, "cells"),
        P(None, "cells"),
        P("cells", "lanes"),
        P(None, "cells"),
        P(None, "cells"),
        P("cells"),
        P("cells"),
        P("cells"),
    )
    out_specs = (P(None, "cells"), P("cells"))
    return jax.shard_map(local, mesh=mesh, in_specs=in_specs, out_specs=out_specs, check_vma=False)
```

profile of v0, /device:TPU:1, one launch (start us, length us, event | category | flops | bytes accessed | tf_op | source)
XLA Modules:
  0.0 145.3 jit_solution(13620284711235304744)
XLA Ops:
  0.6 0.8 pad_maximum_fusion
  1.4 9.8 %collective-permute-start.3 = (f32[9,1024]{1,0:T(8,128)S(1)}, f32[9,1024]{1,0:T(8,128)S(1)}, u32[]{:S(2)}, u32[]{:S(2)}) collective-permute-start(f32[9,1024]{1,0:T(8,128)S(1)} %pad_maximum_fusion), channel_id=1, source_target_pairs={{4,0},{6,2},{8,4},{10,6},{12,8},{14,10},{16,12},{18,14},{20,16},{2... | collective-permute-start | bytes 110600 | tf_op jit(solution)/shard_map/ppermute | solution.py:19
  11.3 1.0 collective-permute-start.2
  12.2 0.8 collective-permute-start.1
  13.0 0.7 compare_and_fusion.3
  13.7 0.7 compare_select_fusion.4
  14.3 0.7 multiply_reduce_fusion.1
  15.1 0.8 fusion.38
  15.9 0.8 compare_reduce_fusion
  16.7 0.7 compare_and_fusion.4
  17.4 0.8 copy.114
  18.2 3.0 %collective-permute-done = f32[9,1024]{1,0:T(8,128)S(1)} collective-permute-done((f32[9,1024]{1,0:T(8,128)S(1)}, f32[9,1024]{1,0:T(8,128)S(1)}, u32[]{:S(2)}, u32[]{:S(2)}) %collective-permute-start) | collective-permute-done | bytes 36896 | tf_op jit(solution)/shard_map/ppermute | solution.py:19
  21.2 0.8 constant_dynamic-update-slice_fusion.2
  22.2 28.7 %while.11 = (s32[]{:T(128)}, f32[3,8,128]{2,0,1:T(4,128)S(1)}, s32[8,8]{1,0:T(8,128)S(1)}, f32[9,40,128]{2,0,1:T(8,128)S(1)}, f32[9,8,128]{2,0,1:T(8,128)S(1)}, /*index=5*/s32[]{:T(128)}, s32[]{:T(128)}) while((s32[]{:T(128)}, f32[3,8,128]{2,0,1:T(4,128)S(1)}, s32[8,8]{1,0:T(8,128)S(1)}, f32[9,40,128]{2,0,1:T(8,128)S(1)}, ...), condition=%wide.region_2.3_spmd.clone, body=%wide.region_0.2_spmd.clone.sunk | while | flops 15781963 | bytes 4129047 | solution.py:62
  22.3 0.6 gather_fusion
  23.6 1.0 fusion.58
  25.8 0.6 gather_fusion
  27.2 1.0 fusion.58
  30.8 1.0 fusion.58
  33.0 0.6 gather_fusion
  34.4 1.0 fusion.58
  36.6 0.6 gather_fusion
  38.0 1.0 fusion.58
  40.2 0.6 gather_fusion
  41.6 1.0 fusion.58
  45.1 1.0 fusion.58
  48.7 1.0 fusion.58
  50.9 4.9 %all_gather.3 = f32[2,3,1024]{2,1,0:T(4,128)S(1)} all-gather(f32[1,3,1024]{2,1,0:T(4,128)S(1)} %bitcast.98), channel_id=1, replica_groups=mesh['cells'=128,'lanes'=2] {'lanes'}, dimensions={0}, use_global_device_ids=true | all-gather | bytes 36864 | tf_op jit(solution)/shard_map/all_gather | solution.py:23
  56.1 6.2 %scatter_custom_fusion.2 = f32[1024,4]{1,0:T(8,128)S(1)} fusion(s32[1024]{0:T(1024)S(1)} %bitcast.103, f32[1024,4]{1,0:T(8,128)S(1)} %copy.120, f32[]{:T(128)} %constant.50.clone.1), kind=kCustom, calls=%fused_computation.67 | custom fusion | flops 4096 | bytes 16388 | tf_op jit(solution)/shard_map/scatter-add | solution.py:86
  62.4 6.2 %scatter_custom_fusion.3 = f32[1024,4]{1,0:T(8,128)S(1)} fusion(s32[1024]{0:T(1024)S(1)} %bitcast.107, f32[1024,4]{1,0:T(8,128)S(1)} %copy.121, f32[]{:T(128)} %constant.50.clone.1), kind=kCustom, calls=%fused_computation.65 | custom fusion | flops 4096 | bytes 16388 | tf_op jit(solution)/shard_map/scatter-add | solution.py:86
  69.2 6.1 %scatter_custom_fusion.1 = f32[1024,4]{1,0:T(8,128)S(1)} fusion(s32[1024]{0:T(1024)S(1)} %bitcast.108, f32[1024,4]{1,0:T(8,128)S(1)} %copy.119, f32[]{:T(128)} %constant.50.clone.1), kind=kCustom, calls=%fused_computation.69 | custom fusion | flops 4096 | bytes 16388 | tf_op jit(solution)/shard_map/scatter-add | solution.py:86
  75.6 6.2 %scatter_custom_fusion = f32[1024,4]{1,0:T(8,128)S(1)} fusion(s32[1024]{0:T(1024)S(1)} %bitcast.104, f32[1024,4]{1,0:T(8,128)S(1)} %copy.118, f32[]{:T(128)} %constant.50.clone.1), kind=kCustom, calls=%fused_computation.71 | custom fusion | flops 4096 | bytes 16388 | tf_op jit(solution)/shard_map/scatter-add | solution.py:86
  82.6 1.8 %collective-permute-start.5 = (f32[3,1024]{0,1:T(8,128)S(1)}, f32[3,1024]{0,1:T(8,128)S(1)}, u32[]{:S(2)}, u32[]{:S(2)}) collective-permute-start(f32[3,1024]{0,1:T(8,128)S(1)} %fusion.22), channel_id=1, source_target_pairs={{2,0},{4,2},{6,4},{8,6},{10,8},{12,10},{14,12},{16,14},{18,16},{20... | collective-permute-start | bytes 36872 | tf_op jit(solution)/shard_map/ppermute | solution.py:19
  84.4 0.8 copy.132
  85.2 2.8 %gather_fusion.5 = f32[1024,3]{1,0:T(8,128)S(1)} fusion(f32[3,1024]{0,1:T(8,128)S(1)} %fusion.22, s32[1024]{0:T(1024)S(1)} %get-tuple-element.126), kind=kCustom, calls=%fused_computation.3.clone | custom fusion | bytes 28672 | tf_op jit(solution)/shard_map/jit(_take)/gather | solution.py:93
  88.0 2.8 %gather_fusion.3 = f32[1024,3]{1,0:T(8,128)S(1)} fusion(f32[3,1024]{0,1:T(8,128)S(1)} %fusion.22, s32[1024]{0:T(1024)S(1)} %get-tuple-element.125), kind=kCustom, calls=%fused_computation.1.clone | custom fusion | bytes 28672 | tf_op jit(solution)/shard_map/jit(_take)/gather | solution.py:93
  91.2 2.8 %gather_fusion.6 = f32[1024,3]{1,0:T(8,128)S(1)} fusion(f32[3,1024]{0,1:T(8,128)S(1)} %collective-permute-done.5, s32[1024]{0:T(1024)S(1)} %get-tuple-element.126), kind=kCustom, calls=%fused_computation.4.clone | custom fusion | bytes 28672 | tf_op jit(solution)/shard_map/jit(_take)/gather | solution.py:94
  94.1 2.8 %gather_fusion.4 = f32[1024,3]{1,0:T(8,128)S(1)} fusion(f32[3,1024]{0,1:T(8,128)S(1)} %collective-permute-done.5, s32[1024]{0:T(1024)S(1)} %get-tuple-element.125), kind=kCustom, calls=%fused_computation.2.clone | custom fusion | bytes 28672 | tf_op jit(solution)/shard_map/jit(_take)/gather | solution.py:94
  96.9 0.9 fusion.24
  98.0 11.5 %collective-permute-start.9 = (f32[3,1024]{0,1:T(8,128)S(1)}, f32[3,1024]{0,1:T(8,128)S(1)}, u32[]{:S(2)}, u32[]{:S(2)}) collective-permute-start(f32[3,1024]{0,1:T(8,128)S(1)} %fusion.24), channel_id=1, source_target_pairs={{4,0},{6,2},{8,4},{10,6},{12,8},{14,10},{16,12},{18,14},{20,16},{2... | collective-permute-start | bytes 36872 | tf_op jit(solution)/shard_map/ppermute | solution.py:19
  109.5 1.7 %collective-permute-start.7 = (f32[3,1024]{0,1:T(8,128)S(1)}, f32[3,1024]{0,1:T(8,128)S(1)}, u32[]{:S(2)}, u32[]{:S(2)}) collective-permute-start(f32[3,1024]{0,1:T(8,128)S(1)} %fusion.24), channel_id=1, source_target_pairs={{254,0},{0,2},{2,4},{4,6},{6,8},{8,10},{10,12},{12,14},{14,16},{16... | collective-permute-start | bytes 36872 | tf_op jit(solution)/shard_map/ppermute | solution.py:19
  111.3 0.6 gather_fusion.1
  112.1 21.3 %collective-permute-done.6 = f32[3,1024]{0,1:T(8,128)S(1)} collective-permute-done((f32[3,1024]{0,1:T(8,128)S(1)}, f32[3,1024]{0,1:T(8,128)S(1)}, u32[]{:S(2)}, u32[]{:S(2)}) %collective-permute-start.6) | collective-permute-done | bytes 12320 | tf_op jit(solution)/shard_map/ppermute | solution.py:19
  134.3 0.6 gather_fusion.2
  135.1 4.2 %fusion.18 = (f32[32,128,128]{2,1,0:T(8,128)S(1)}, f32[32,128,128]{2,1,0:T(8,128)S(1)}) fusion(f32[3,32,128]{2,1,0:T(8,128)S(1)} %copy.131, f32[3,32,128]{2,1,0:T(8,128)S(1)} %copy.130, f32[3,32,128]{2,1,0:T(8,128)S(1)} %copy.129, f32[3,32,128]{2,1,0:T(8,128)S(1)} %copy.123), kind=kLoop, calls=%fused_computation.49 | loop fusion | flops 9961472 | bytes 4390912 | tf_op jit(solution)/shard_map/reduce_sum | solution.py:71
  139.8 4.1 %fusion.20 = f32[32,128,128]{2,1,0:T(8,128)S(1)} fusion(f32[32,128,128]{2,1,0:T(8,128)S(1)} %clamp_multiply_fusion, f32[3,32,128]{2,1,0:T(8,128)S(1)} %copy.131, f32[3,32,128]{2,1,0:T(8,128)S(1)} %copy.130, f32[3,32,128]{2,1,0:T(8,128)S(1)} %copy.129, f32[3,32,128]{2,1,0:T(8,128)S(1)} %copy.123), kind=kLoop, calls=%fused_computation.51 | loop fusion | flops 8912896 | bytes 4390912 | tf_op jit(solution)/shard_map/reduce_sum | solution.py:75
  143.9 0.6 exponential_reduce_fusion
  144.5 0.9 convolution_bitcast_fusion.3
  (184 shorter events, 21.5 us)
Async XLA Ops:
  1.4 20.6 %collective-permute-start.3 = (f32[9,1024]{1,0:T(8,128)S(1)}, f32[9,1024]{1,0:T(8,128)S(1)}, u32[]{:S(2)}, u32[]{:S(2)}) collective-permute-start(f32[9,1024]{1,0:T(8,128)S(1)} %pad_maximum_fusion), channel_id=1, source_target_pairs={{4,0},{6,2},{8,4},{10,6},{12,8},{14,10},{16,12},{18,14},{20,16},{2... | collective-permute-start | bytes 110600 | tf_op jit(solution)/shard_map/ppermute | solution.py:19
  11.3 10.7 %collective-permute-start.2 = (f32[9,1024]{1,0:T(8,128)S(1)}, f32[9,1024]{1,0:T(8,128)S(1)}, u32[]{:S(2)}, u32[]{:S(2)}) collective-permute-start(f32[9,1024]{1,0:T(8,128)S(1)} %pad_maximum_fusion), channel_id=1, source_target_pairs={{2,0},{4,2},{6,4},{8,6},{10,8},{12,10},{14,12},{16,14},{18,16},{20... | collective-permute-start | bytes 110600 | tf_op jit(solution)/shard_map/ppermute | solution.py:19
  12.2 9.0 %collective-permute-start.1 = (f32[9,1024]{1,0:T(8,128)S(1)}, f32[9,1024]{1,0:T(8,128)S(1)}, u32[]{:S(2)}, u32[]{:S(2)}) collective-permute-start(f32[9,1024]{1,0:T(8,128)S(1)} %pad_maximum_fusion), channel_id=1, source_target_pairs={{254,0},{0,2},{2,4},{4,6},{6,8},{8,10},{10,12},{12,14},{14,16},{16... | collective-permute-start | bytes 110600 | tf_op jit(solution)/shard_map/ppermute | solution.py:19
  13.0 8.2 %collective-permute-start = (f32[9,1024]{1,0:T(8,128)S(1)}, f32[9,1024]{1,0:T(8,128)S(1)}, u32[]{:S(2)}, u32[]{:S(2)}) collective-permute-start(f32[9,1024]{1,0:T(8,128)S(1)} %pad_maximum_fusion), channel_id=1, source_target_pairs={{252,0},{254,2},{0,4},{2,6},{4,8},{6,10},{8,12},{10,14},{12,16},{1... | collective-permute-start | bytes 110600 | tf_op jit(solution)/shard_map/ppermute | solution.py:19
  50.9 18.1 %copy-start.2 = (s32[32]{0:T(128)S(1)}, s32[32]{0:T(128)}, u32[]{:S(2)}) copy-start(s32[32]{0:T(128)} %param.20) | copy-start | bytes 388
  68.7 13.1 %collective-permute-start.4 = (f32[4,1024]{0,1:T(8,128)S(1)}, f32[4,1024]{0,1:T(8,128)S(1)}, u32[]{:S(2)}, u32[]{:S(2)}) collective-permute-start(f32[4,1024]{0,1:T(8,128)S(1)} %add_bitcast_fusion), channel_id=1, source_target_pairs={{254,0},{0,2},{2,4},{4,6},{6,8},{8,10},{10,12},{12,14},{14,16},{16... | collective-permute-start | bytes 49160 | tf_op jit(solution)/shard_map/ppermute | solution.py:19
  69.2 13.0 %copy-start.1 = (f32[1024]{0:T(1024)S(1)}, f32[1024]{0:T(1024)}, u32[]{:S(2)}) copy-start(f32[1024]{0:T(1024)} %param.19) | copy-start | bytes 12292
  82.6 8.7 %collective-permute-start.5 = (f32[3,1024]{0,1:T(8,128)S(1)}, f32[3,1024]{0,1:T(8,128)S(1)}, u32[]{:S(2)}, u32[]{:S(2)}) collective-permute-start(f32[3,1024]{0,1:T(8,128)S(1)} %fusion.22), channel_id=1, source_target_pairs={{2,0},{4,2},{6,4},{8,6},{10,8},{12,10},{14,12},{16,14},{18,16},{20... | collective-permute-start | bytes 36872 | tf_op jit(solution)/shard_map/ppermute | solution.py:19
  84.4 26.9 %copy-start = (f32[3,1024]{1,0:T(4,128)S(1)}, f32[3,1024]{1,0:T(4,128)}, u32[]{:S(2)}) copy-start(f32[3,1024]{1,0:T(4,128)} %param.13) | copy-start | bytes 36868
  98.0 36.0 %collective-permute-start.9 = (f32[3,1024]{0,1:T(8,128)S(1)}, f32[3,1024]{0,1:T(8,128)S(1)}, u32[]{:S(2)}, u32[]{:S(2)}) collective-permute-start(f32[3,1024]{0,1:T(8,128)S(1)} %fusion.24), channel_id=1, source_target_pairs={{4,0},{6,2},{8,4},{10,6},{12,8},{14,10},{16,12},{18,14},{20,16},{2... | collective-permute-start | bytes 36872 | tf_op jit(solution)/shard_map/ppermute | solution.py:19
  109.5 24.3 %collective-permute-start.8 = (f32[3,1024]{0,1:T(8,128)S(1)}, f32[3,1024]{0,1:T(8,128)S(1)}, u32[]{:S(2)}, u32[]{:S(2)}) collective-permute-start(f32[3,1024]{0,1:T(8,128)S(1)} %fusion.24), channel_id=1, source_target_pairs={{2,0},{4,2},{6,4},{8,6},{10,8},{12,10},{14,12},{16,14},{18,16},{20... | collective-permute-start | bytes 36872 | tf_op jit(solution)/shard_map/ppermute | solution.py:19
  109.5 24.0 %collective-permute-start.7 = (f32[3,1024]{0,1:T(8,128)S(1)}, f32[3,1024]{0,1:T(8,128)S(1)}, u32[]{:S(2)}, u32[]{:S(2)}) collective-permute-start(f32[3,1024]{0,1:T(8,128)S(1)} %fusion.24), channel_id=1, source_target_pairs={{254,0},{0,2},{2,4},{4,6},{6,8},{8,10},{10,12},{12,14},{14,16},{16... | collective-permute-start | bytes 36872 | tf_op jit(solution)/shard_map/ppermute | solution.py:19
  111.3 22.1 %collective-permute-start.6 = (f32[3,1024]{0,1:T(8,128)S(1)}, f32[3,1024]{0,1:T(8,128)S(1)}, u32[]{:S(2)}, u32[]{:S(2)}) collective-permute-start(f32[3,1024]{0,1:T(8,128)S(1)} %fusion.24), channel_id=1, source_target_pairs={{252,0},{254,2},{0,4},{2,6},{4,8},{6,10},{8,12},{10,14},{12,16},{1... | collective-permute-start | bytes 36872 | tf_op jit(solution)/shard_map/ppermute | solution.py:19
where the time goes:
time: 148 us; the launch traced here: 145 us
  other arithmetic  46.2 us (31%)
  starting transfers between devices  27 us (18%)
  waiting for transfers between devices  24.7 us (17%)
  local copies, waits for them, and re-layouts  23 us (16%)
  matrix products  17.6 us (12%)
  blocking collectives  4.89 us (3%)
    ppermute x10, starting transfers between devices, passed_along(): return lax.ppermute(block, axis, route)  27 us
    ppermute x10, waiting for transfers between devices, passed_along(): return lax.ppermute(block, axis, route)  24.7 us
    scatter-add x4, other arithmetic, deposit(): jax.ops.segment_sum(jnp.transpose(masked), node_ids, num_segments=node_co...  24.6 us
    dot_general x8, matrix products, tile_forces(): jnp.einsum('ckj,cki->kij', source_burgers, target_line, precision=HIGH)  8.18 us
    gather x2, local copies, waits for them, and re-layouts, end_velocity(): jnp.take(next_velocity, node_ids, axis=1)  5.61 us
    gather x2, local copies, waits for them, and re-layouts, end_velocity(): jnp.take(velocity, node_ids, axis=1)  5.61 us
    all_gather x1, blocking collectives, total_of_pieces(): parts = lax.all_gather(array, axis)  4.89 us
    gather x8, local copies, waits for them, and re-layouts, add_entry(): chosen = jnp.take(window_blocks, column, axis=1)  4.44 us
  transfers between devices with their start and end apart: 10, of which 3 were waited for; matrix products, arithmetic and copies ran while one was open for 18% of the time, Pallas kernels for 0%

commit v1 on v0

v1 whole, which is shorter than its diff:
```python
import functools

import jax
import jax.numpy as jnp
from jax import lax
from jax.experimental import pallas as pl
from jax.experimental.pallas import tpu as pltpu
from jax.sharding import PartitionSpec as P

BLK = 128
NB = 8
SEG = BLK * NB
HALF = NB // 2
NENT = 8
NCAND = 32
WIDE = 2
FAR = 3
SPAN = 2 * FAR + 1
FORCE_SCALE = 0.02
CORE_SQUARE = 0.25
TIME_STEP = 4.0
CENTRE = 2.0
F32 = jnp.float32
BF16 = jnp.bfloat16
MESH = pl.DeviceIdType.MESH
NT = (((1,), (1,)), ((), ()))
NN = (((1,), (0,)), ((), ()))


def rounded(x):
    return x.astype(BF16).astype(F32)


def two_parts(x):
    top = rounded(x)
    return top, rounded(x - top)


def three_parts(x):
    top = rounded(x)
    rest = x - top
    mid = rounded(rest)
    return top, mid, rounded(rest - mid)


def kernel(
    n_cells,
    lists_hbm,
    cand_t,
    cand_s,
    centres_hbm,
    lines_hbm,
    burgers_hbm,
    nodes_hbm,
    owner_hbm,
    mobility,
    velocity_out,
    nearness_out,
    win_c,
    win_l,
    win_b,
    codes_n,
    codes_o,
    list_own,
    list_far_v,
    list_far,
    feat,
    tall,
    feat_q,
    feat_a,
    pull,
    tgt_q,
    tgt_a,
    onehot,
    mask16,
    drag_send,
    drag_recv,
    eff,
    fbuf,
    vel,
    mot,
    local_sem,
    send_a,
    recv_a,
    send_n,
    recv_n,
    misc_sem,
    send_b,
    recv_b,
):
    me = lax.axis_index("cells")
    lane = lax.axis_index("lanes")
    other = 1 - lane

    def cell(offset):
        return lax.rem(me + (offset + n_cells), n_cells)

    partners = [
        (o, far) for o in (0, 1, -1, 2, -2, 3, -3) for far in (False, True) if (o, far) != (0, False)
    ]

    barrier = pltpu.get_barrier_semaphore()
    for o, far in partners:
        pl.semaphore_signal(
            barrier, inc=1, device_id=(cell(o), other if far else lane), device_id_type=MESH
        )
    own_copies = [
        pltpu.make_async_copy(centres_hbm, win_c.at[WIDE], local_sem.at[0]),
        pltpu.make_async_copy(lines_hbm, win_l.at[WIDE], local_sem.at[1]),
        pltpu.make_async_copy(burgers_hbm, win_b.at[WIDE], local_sem.at[2]),
        pltpu.make_async_copy(nodes_hbm, codes_n.at[FAR], local_sem.at[3]),
        pltpu.make_async_copy(owner_hbm, codes_o.at[FAR], local_sem.at[4]),
        pltpu.make_async_copy(lists_hbm, list_own, local_sem.at[5]),
    ]
    for copy in own_copies:
        copy.start()
    pl.semaphore_wait(barrier, len(partners))

    def remote(src, dst, send, recv, o, far):
        return pltpu.make_async_remote_copy(
            src_ref=src,
            dst_ref=dst,
            send_sem=send,
            recv_sem=recv,
            device_id=(cell(o), other if far else lane),
            device_id_type=MESH,
        )

    sends_a = {}
    for o in (1, -1, 2, -2):
        for a, (src, dst) in enumerate(
            ((centres_hbm, win_c), (lines_hbm, win_l), (burgers_hbm, win_b))
        ):
            slot = WIDE - o
            sends_a[(o, a)] = remote(
                src, dst.at[slot], send_a.at[WIDE + o, a], recv_a.at[slot, a], o, False
            )
            sends_a[(o, a)].start()
    list_copy = remote(lists_hbm, list_far_v, misc_sem.at[0], misc_sem.at[1], 0, True)
    list_copy.start()
    sends_n = {}
    for o in (1, -1, 2, -2, 3, -3):
        for a, (src, dst) in enumerate(((nodes_hbm, codes_n), (owner_hbm, codes_o))):
            slot = FAR - o
            sends_n[(o, a)] = remote(
                src, dst.at[slot], send_n.at[FAR + o, a], recv_n.at[slot, a], o, False
            )
            sends_n[(o, a)].start()
    for copy in own_copies:
        copy.wait()

    def build_codes(slot):
        for e in range(2):
            node = codes_n[slot, e : e + 1, :] + SEG * codes_o[slot, e : e + 1, :]
            low = jnp.bitwise_and(node, BLK - 1)
            high = lax.shift_right_logical(node, 7)
            span = pl.ds(e * SEG, SEG)
            rows = lax.broadcasted_iota(jnp.int32, (BLK, SEG), 0)
            onehot[slot, :, span] = (rows == low).astype(F32).astype(BF16)
            rows16 = lax.broadcasted_iota(jnp.int32, (16, SEG), 0)
            mask16[slot, :, span] = (rows16 == high).astype(F32)

    feat[...] = jnp.zeros_like(feat)

    def build_source(s):
        c = win_c[s] - CENTRE
        ch, cm, cl = three_parts(c)
        for g, part in enumerate((ch, cm, ch, cm, cl, ch)):
            feat[8 * g : 8 * g + 3, :] = part
        rows = [win_c[s, k : k + 1, :] - CENTRE for k in range(3)]
        square = rows[0] * rows[0] + rows[1] * rows[1] + rows[2] * rows[2] + CORE_SQUARE
        for k, part in enumerate(three_parts(square)):
            feat[48 + k : 49 + k, :] = part
            feat[51 + k : 52 + k, :] = jnp.ones_like(part)
        bh, bm, bl = three_parts(win_b[s])
        for g, part in enumerate((bh, bm, bh, bm, bl, bh)):
            feat[64 + 8 * g : 64 + 8 * g + 3, :] = part
        line = [win_l[s, k : k + 1, :] for k in range(3)]
        moment = (
            line[1] * rows[2] - line[2] * rows[1],
            line[2] * rows[0] - line[0] * rows[2],
            line[0] * rows[1] - line[1] * rows[0],
        )
        for k in range(3):
            lh, ll = two_parts(line[k])
            mh, ml = two_parts(moment[k])
            for g, part in enumerate((lh, mh, ll, ml)):
                tall[8 * g + k : 8 * g + k + 1, :] = part
        for b in range(NB):
            cut = slice(b * BLK, (b + 1) * BLK)
            feat_q[s * NB + b] = feat[0:64, cut].astype(BF16)
            feat_a[s * NB + b] = feat[64:128, cut].astype(BF16)
            pull[s * NB + b] = tall[:, cut].astype(BF16)
            mot[s * NB + b, 0:3, :] = win_c[s, :, cut]

    tall[...] = jnp.zeros_like(tall)
    build_source(WIDE)

    c = win_c[WIDE] - CENTRE
    ch, cm, cl = three_parts(c)
    for g, part in enumerate((ch, ch, cm, cm, ch, cl)):
        feat[8 * g : 8 * g + 3, :] = -2.0 * part
    rows = [win_c[WIDE, k : k + 1, :] - CENTRE for k in range(3)]
    square = rows[0] * rows[0] + rows[1] * rows[1] + rows[2] * rows[2]
    for k, part in enumerate(three_parts(square)):
        feat[51 + k : 52 + k, :] = part
        feat[48 + k : 49 + k, :] = jnp.ones_like(part)
    lh, lm, ll = three_parts(win_l[WIDE])
    for g, part in enumerate((lh, lh, lm, lm, lh, ll)):
        feat[64 + 8 * g : 64 + 8 * g + 3, :] = part
    for b in range(NB):
        cut = slice(b * BLK, (b + 1) * BLK)
        turned = jnp.transpose(feat[:, cut])
        tgt_q[b] = turned[:, 0:64].astype(BF16)
        tgt_a[b] = turned[:, 64:128].astype(BF16)

    build_codes(FAR)
    line = [win_l[WIDE, k : k + 1, :] for k in range(3)]
    length = 0.5 * jnp.sqrt(line[0] * line[0] + line[1] * line[1] + line[2] * line[2])
    drag = jnp.zeros((32, BLK), F32)
    for e in range(2):
        span = slice(e * SEG, (e + 1) * SEG)
        mask = mask16[FAR, :, span] > 0.5
        parts = [
            jnp.where(mask, jnp.broadcast_to(part, (16, SEG)), 0.0) for part in two_parts(length)
        ]
        drag = drag + lax.dot_general(
            jnp.concatenate(parts, axis=0).astype(BF16),
            onehot[FAR, :, span],
            NT,
            preferred_element_type=F32,
        )
    drag_send[...] = drag[8:16] + drag[24:32]
    drag_copy = remote(drag_send, drag_recv, misc_sem.at[2], misc_sem.at[3], 1, False)
    drag_copy.start()
    own_drag = drag[0:8] + drag[16:24]

    for o in (1, -1, 2, -2):
        for a in range(3):
            sends_a[(-o, a)].wait_recv()
        build_source(WIDE + o)
    list_copy.wait_recv()
    to_smem = pltpu.make_async_copy(list_far_v, list_far, misc_sem.at[4])
    to_smem.start()
    to_smem.wait()
    drag_copy.wait_recv()
    eff_all = mobility[...] / (1.0 + (own_drag + drag_recv[...]))
    for b in range(NB):
        eff[b] = eff_all[b : b + 1, :]

    def one_target(t, carry):
        block = HALF * lane + t
        left_q = tgt_q[block]
        left_a = tgt_a[block]
        total = jnp.zeros((32, BLK), F32)
        for lists in (list_own, list_far):
            for e in range(NENT):
                source = lists[block, e]
                q = lax.dot_general(left_q, feat_q[source], NN, preferred_element_type=F32)
                along = lax.dot_general(left_a, feat_a[source], NN, preferred_element_type=F32)
                inverse = lax.rsqrt(q)
                weight = along * inverse * inverse * inverse
                top = weight.astype(BF16)
                low = (weight - top.astype(F32)).astype(BF16)
                pulls = pull[source]
                total = total + lax.dot_general(pulls, top, NT, preferred_element_type=F32)
                total = total + lax.dot_general(pulls, low, NT, preferred_element_type=F32)
        total = total[0:16] + total[16:32]
        cut = pl.ds(pl.multiple_of(block * BLK, BLK), BLK)
        x, y, z = (win_c[WIDE, k : k + 1, cut] - CENTRE for k in range(3))
        sx, sy, sz = (total[k : k + 1] for k in range(3))
        scale = 0.5 * FORCE_SCALE
        fbuf[FAR, block, 0:1, :] = scale * (sy * z - sz * y - total[8:9])
        fbuf[FAR, block, 1:2, :] = scale * (sz * x - sx * z - total[9:10])
        fbuf[FAR, block, 2:3, :] = scale * (sx * y - sy * x - total[10:11])
        fbuf[FAR, block, 3:4, :] = eff[block]
        return carry

    lax.fori_loop(0, HALF, one_target, 0)

    mine = pl.ds(HALF * lane, HALF)
    sends_b = []
    for o, far in partners:
        slot = FAR - o
        copy = remote(
            fbuf.at[FAR, mine],
            fbuf.at[slot, mine],
            send_b.at[FAR + o, int(far)],
            recv_b.at[slot, int(far)],
            o,
            far,
        )
        copy.start()
        sends_b.append(copy)

    for o in (1, -1, 2, -2, 3, -3):
        for a in range(2):
            sends_n[(-o, a)].wait_recv()
        build_codes(FAR + o)

    own_part = {}
    next_part = {}
    recv_of = {(o, far): copy for (o, far), copy in zip(partners, sends_b)}
    for o in (0, 1, -1, 2, -2, 3, -3):
        slot = FAR + o
        for far in (False, True):
            if (-o, far) in recv_of:
                recv_of[(-o, far)].wait_recv()
        forces = jnp.concatenate([fbuf[slot, b] for b in range(NB)], axis=1)
        parts = two_parts(forces)
        total = jnp.zeros((96, BLK), F32)
        for e in range(2):
            span = slice(e * SEG, (e + 1) * SEG)
            mask = mask16[slot, :, span] > 0.5
            stack = [
                jnp.where(mask, jnp.broadcast_to(part[k : k + 1], (16, SEG)), 0.0)
                for part in parts
                for k in range(3)
            ]
            total = total + lax.dot_general(
                jnp.concatenate(stack, axis=0).astype(BF16),
                onehot[slot, :, span],
                NT,
                preferred_element_type=F32,
            )
        total = total[0:48] + total[48:96]
        own_part[o] = [total[16 * k : 16 * k + 8] for k in range(3)]
        next_part[o] = [total[16 * k + 8 : 16 * k + 16] for k in range(3)]

    for o in range(-WIDE, FAR + 1):
        eff_o = jnp.concatenate([fbuf[FAR + o, b, 3:4, :] for b in range(NB)], axis=0)
        for k in range(3):
            value = eff_o * (own_part[o][k] + next_part[o - 1][k])
            vel[FAR + o, k] = value
            if o == 0:
                for b in range(NB):
                    velocity_out[k : k + 1, b * BLK : (b + 1) * BLK] = value[b : b + 1, :]

    for o in range(-WIDE, WIDE + 1):
        slot = FAR + o
        table = jnp.concatenate(
            [piece for k in range(3) for piece in (vel[slot, k], vel[slot + 1, k])], axis=0
        )
        stack = jnp.concatenate(two_parts(table), axis=0).astype(BF16)
        both = None
        for e in range(2):
            span = slice(e * SEG, (e + 1) * SEG)
            picked = lax.dot_general(stack, onehot[slot, :, span], NN, preferred_element_type=F32)
            picked = picked[0:48] + picked[48:96]
            mask = mask16[slot, :, span] > 0.5
            kept = [jnp.where(mask, picked[16 * k : 16 * k + 16], 0.0) for k in range(3)]
            both = kept if both is None else [x + y for x, y in zip(both, kept)]
        for k in range(3):
            row = 0.5 * TIME_STEP * jnp.sum(both[k], axis=0, keepdims=True)
            for b in range(NB):
                mot[(WIDE + o) * NB + b, 3 + k : 4 + k, :] = row[:, b * BLK : (b + 1) * BLK]

    block_rows = lax.broadcasted_iota(jnp.int32, (NB, BLK), 0)

    def one_pair(n, near):
        target = cand_t[n]
        source = cand_s[n]
        here = mot[WIDE * NB + target]
        there = jnp.transpose(mot[source])
        goal = [jnp.broadcast_to(here[k : k + 1], (8, BLK)) for k in range(6)]
        total = jnp.zeros((8, BLK), F32)
        for r in range(BLK // 8):
            chunk = there[8 * r : 8 * r + 8]
            gap = [goal[k] - jnp.broadcast_to(chunk[:, k : k + 1], (8, BLK)) for k in range(6)]
            x, y, z, u, v, w = gap
            approach = x * u + y * v + z * w
            square = u * u + v * v + w * w
            fraction = jnp.clip(-approach / (square + CORE_SQUARE), 0.0, 1.0)
            x = x + fraction * u
            y = y + fraction * v
            z = z + fraction * w
            total = total + jnp.exp(-(x * x + y * y + z * z))
        row = jnp.sum(total, axis=0, keepdims=True)
        return near + jnp.where(block_rows == target, jnp.broadcast_to(row, (NB, BLK)), 0.0)

    nearness_out[...] = lax.fori_loop(0, NCAND, one_pair, jnp.zeros((NB, BLK), F32))

    for copy in list(sends_a.values()) + list(sends_n.values()) + sends_b + [list_copy, drag_copy]:
        copy.wait_send()


def local(
    centres,
    seg_lines,
    burgers,
    neighbour_blocks,
    seg_nodes,
    node_owner,
    mobility,
    cand_target,
    cand_source,
):
    n_cells = lax.axis_size("cells")
    window = 2 * WIDE + 1
    anywhere = pl.BlockSpec(memory_space=pl.ANY)
    vmem = pl.BlockSpec(memory_space=pltpu.VMEM)
    smem = pl.BlockSpec(memory_space=pltpu.SMEM)
    velocity, nearness = pl.pallas_call(
        functools.partial(kernel, n_cells),
        name="dislocation_step",
        out_shape=(
            jax.ShapeDtypeStruct((3, SEG), F32),
            jax.ShapeDtypeStruct((NB, BLK), F32),
        ),
        in_specs=[anywhere, smem, smem] + [anywhere] * 5 + [vmem],
        out_specs=(vmem, vmem),
        scratch_shapes=[
            pltpu.VMEM((window, 3, SEG), F32),
            pltpu.VMEM((window, 3, SEG), F32),
            pltpu.VMEM((window, 3, SEG), F32),
            pltpu.VMEM((SPAN, 2, SEG), jnp.int32),
            pltpu.VMEM((SPAN, 2, SEG), jnp.int32),
            pltpu.SMEM((NB, NENT), jnp.int32),
            pltpu.VMEM((NB, NENT), jnp.int32),
            pltpu.SMEM((NB, NENT), jnp.int32),
            pltpu.VMEM((128, SEG), F32),
            pltpu.VMEM((32, SEG), F32),
            pltpu.VMEM((window * NB, 64, BLK), BF16),
            pltpu.VMEM((window * NB, 64, BLK), BF16),
            pltpu.VMEM((window * NB, 32, BLK), BF16),
            pltpu.VMEM((NB, BLK, 64), BF16),
            pltpu.VMEM((NB, BLK, 64), BF16),
            pltpu.VMEM((SPAN, BLK, 2 * SEG), BF16),
            pltpu.VMEM((SPAN, 16, 2 * SEG), F32),
            pltpu.VMEM((NB, BLK), F32),
            pltpu.VMEM((NB, BLK), F32),
            pltpu.VMEM((NB, 1, BLK), F32),
            pltpu.VMEM((SPAN, NB, 4, BLK), F32),
            pltpu.VMEM((SPAN, 3, NB, BLK), F32),
            pltpu.VMEM((window * NB, 8, BLK), F32),
            pltpu.SemaphoreType.DMA((6,)),
            pltpu.SemaphoreType.DMA((window, 3)),
            pltpu.SemaphoreType.DMA((window, 3)),
            pltpu.SemaphoreType.DMA((SPAN, 2)),
            pltpu.SemaphoreType.DMA((SPAN, 2)),
            pltpu.SemaphoreType.DMA((5,)),
            pltpu.SemaphoreType.DMA((SPAN, 2)),
            pltpu.SemaphoreType.DMA((SPAN, 2)),
        ],
        compiler_params=pltpu.CompilerParams(
            collective_id=0, has_side_effects=True, vmem_limit_bytes=40 * 2**20
        ),
    )(
        neighbour_blocks,
        cand_target,
        cand_source,
        centres,
        seg_lines,
        burgers,
        seg_nodes,
        node_owner,
        mobility.reshape(NB, BLK),
    )
    return velocity, nearness.reshape(SEG)


def solution(mesh):
    in_specs = (
        P(None, "cells"),
        P(None, "cells"),
        P(None, "cells"),
        P("cells", "lanes"),
        P(None, "cells"),
        P(None, "cells"),
        P("cells"),
        P("cells"),
        P("cells"),
    )
    out_specs = (P(None, "cells"), P("cells"))
    return jax.shard_map(local, mesh=mesh, in_specs=in_specs, out_specs=out_specs, check_vma=False)
```

time: 148 us -> 53 us (0.36); the launches traced: 145 us -> 52.5 us
  other arithmetic: 46.2 us -> 0 us
  Pallas kernels: 0 us -> 45 us
  starting transfers between devices: 27 us -> 0 us
  waiting for transfers between devices: 24.7 us -> 0 us
  matrix products: 17.6 us -> 0 us
  local copies, waits for them, and re-layouts: 23 us -> 6.77 us
  blocking collectives: 4.89 us -> 0 us
    pallas_call x0 -> x1, Pallas kernels: none -> 45 us  [local(): pl.pallas_call(functools.partial(kernel, n_cells), name='dislocation_step...]
    ppermute x10 -> x0, starting transfers between devices: 27 us -> none  [passed_along(): return lax.ppermute(block, axis, route)]
    ppermute x10 -> x0, waiting for transfers between devices: 24.7 us -> none  [passed_along(): return lax.ppermute(block, axis, route)]
    scatter-add x4 -> x0, other arithmetic: 24.6 us -> none  [deposit(): jax.ops.segment_sum(jnp.transpose(masked), node_ids, num_segments=node_co...]
    dot_general x25 -> x0, matrix products: 17.6 us -> none  [the longest x8 8.18 us: tile_forces(): jnp.einsum('ckj,cki->kij', source_burgers, target_line, precision=HIGH)]
    gather x14 -> x0, local copies, waits for them, and re-layouts: 16.8 us -> none  [the longest x2 5.61 us: end_velocity(): jnp.take(next_velocity, node_ids, axis=1)]
    reduce_sum x13 -> x0, other arithmetic: 13.4 us -> none  [the longest x1 4.18 us: swept_tiles(): approach = jnp.sum(separation * motion, axis=0)]
    unnamed x19 -> x20, local copies, waits for them, and re-layouts: 1.77 us -> 6.77 us
  transfers between devices with their start and end apart: 10 -> 0, of which waited for: 3 -> 0; matrix products, arithmetic and copies ran while one was open for 18% -> 0% of each run, Pallas kernels for 0% -> 0%
where the time goes in v1:
time: 53 us; the launch traced here: 52.5 us
  Pallas kernels  45 us (85%)
  local copies, waits for them, and re-layouts  6.77 us (13%)
  between operations  0.67 us (1%)
    pallas_call x1, Pallas kernels, local(): pl.pallas_call(functools.partial(kernel, n_cells), name='dislocation_step...  45 us
    unnamed x20, local copies, waits for them, and re-layouts  6.77 us

profile of v1, /device:TPU:1, one launch (start us, length us, event | category | flops | bytes accessed | tf_op | source)
XLA Modules:
  0.0 52.5 jit_solution(17579531127342183637)
XLA Ops:
  0.6 0.0 copy-start.8
  0.6 0.0 copy-start.7
  0.7 0.6 %copy-done.8 = s32[32]{0:T(128)S(1)} copy-done((s32[32]{0:T(128)S(1)}, s32[32]{0:T(128)}, u32[]{:S(2)}) %copy-start.8) | copy-done | bytes 152
  1.3 0.0 copy-done.7
  1.3 0.0 copy-start
  1.3 0.7 %copy-done = f32[3,1024]{1,0:T(4,128)S(1)} copy-done((f32[3,1024]{1,0:T(4,128)S(1)}, f32[3,1024]{1,0:T(4,128)}, u32[]{:S(2)}) %copy-start) | copy-done | bytes 12312
  2.0 0.0 copy-start.1
  2.0 0.7 %copy-done.1 = f32[3,1024]{1,0:T(4,128)S(1)} copy-done((f32[3,1024]{1,0:T(4,128)S(1)}, f32[3,1024]{1,0:T(4,128)}, u32[]{:S(2)}) %copy-start.1) | copy-done | bytes 12312
  2.7 0.0 copy-start.2
  2.7 0.7 %copy-done.2 = f32[3,1024]{1,0:T(4,128)S(1)} copy-done((f32[3,1024]{1,0:T(4,128)S(1)}, f32[3,1024]{1,0:T(4,128)}, u32[]{:S(2)}) %copy-start.2) | copy-done | bytes 12312
  3.5 0.0 copy-start.3
  3.5 0.7 %copy-done.3 = s32[2,1024]{1,0:T(2,128)S(1)} copy-done((s32[2,1024]{1,0:T(2,128)S(1)}, s32[2,1024]{1,0:T(2,128)}, u32[]{:S(2)}) %copy-start.3) | copy-done | bytes 8216
  4.2 0.0 copy-start.4
  4.2 0.7 %copy-done.4 = s32[2,1024]{1,0:T(2,128)S(1)} copy-done((s32[2,1024]{1,0:T(2,128)S(1)}, s32[2,1024]{1,0:T(2,128)}, u32[]{:S(2)}) %copy-start.4) | copy-done | bytes 8216
  4.9 0.0 copy-start.5
  4.9 0.7 %copy-done.5 = s32[8,8]{1,0:T(8,128)S(1)} copy-done((s32[8,8]{1,0:T(8,128)S(1)}, s32[8,8]{1,0:T(8,128)}, u32[]{:S(2)}) %copy-start.5) | copy-done | bytes 280
  5.5 0.0 copy-start.6
  5.5 0.7 %copy-done.6 = f32[1024]{0:T(1024)S(1)} copy-done((f32[1024]{0:T(1024)S(1)}, f32[1024]{0:T(1024)}, u32[]{:S(2)}) %copy-start.6) | copy-done | bytes 4120
  6.2 45.0 %dislocation_step.1 = (f32[3,1024]{1,0:T(4,128)S(1)}, f32[8,128]{1,0:T(8,128)S(1)}) custom-call(s32[8,8]{1,0:T(8,128)S(1)} %copy-done.5, s32[32]{0:T(128)S(1)} %copy-done.7, s32[32]{0:T(128)S(1)} %copy-done.8, f32[3,1024]{1,0:T(4,128)S(1)} %copy-done, f32[3,1024]{1,0:T(4,128)S(1)} %copy-done.1, f32[3,1024]{1,0:T(4,128)S(1)} %copy-done.2, ...), custom_call_target="tpu_custom_call" | custom-call | tf_op jit(solution)/shard_map/dislocation_step/pallas_call | solution.py:403
  51.3 0.6 %copy.13 = f32[3,1024]{1,0:T(4,128)} copy(f32[3,1024]{1,0:T(4,128)S(1)} %get-tuple-element.8) | data formatting | bytes 24576
  51.9 0.6 %copy.14 = f32[1024]{0:T(1024)} copy(f32[1024]{0:T(1024)S(1)} %bitcast.3) | data formatting | bytes 8192
Async XLA Ops:
  0.6 0.7 %copy-start.8 = (s32[32]{0:T(128)S(1)}, s32[32]{0:T(128)}, u32[]{:S(2)}) copy-start(s32[32]{0:T(128)} %cand_s.1) | copy-start | bytes 388
  0.6 0.7 %copy-start.7 = (s32[32]{0:T(128)S(1)}, s32[32]{0:T(128)}, u32[]{:S(2)}) copy-start(s32[32]{0:T(128)} %cand_t.1) | copy-start | bytes 388
  1.3 0.7 %copy-start = (f32[3,1024]{1,0:T(4,128)S(1)}, f32[3,1024]{1,0:T(4,128)}, u32[]{:S(2)}) copy-start(f32[3,1024]{1,0:T(4,128)} %centres_hbm.1) | copy-start | bytes 36868
  2.0 0.7 %copy-start.1 = (f32[3,1024]{1,0:T(4,128)S(1)}, f32[3,1024]{1,0:T(4,128)}, u32[]{:S(2)}) copy-start(f32[3,1024]{1,0:T(4,128)} %lines_hbm.1) | copy-start | bytes 36868
  2.7 0.7 %copy-start.2 = (f32[3,1024]{1,0:T(4,128)S(1)}, f32[3,1024]{1,0:T(4,128)}, u32[]{:S(2)}) copy-start(f32[3,1024]{1,0:T(4,128)} %burgers_hbm.1) | copy-start | bytes 36868
  3.5 0.7 %copy-start.3 = (s32[2,1024]{1,0:T(2,128)S(1)}, s32[2,1024]{1,0:T(2,128)}, u32[]{:S(2)}) copy-start(s32[2,1024]{1,0:T(2,128)} %nodes_hbm.1) | copy-start | bytes 24580
  4.2 0.7 %copy-start.4 = (s32[2,1024]{1,0:T(2,128)S(1)}, s32[2,1024]{1,0:T(2,128)}, u32[]{:S(2)}) copy-start(s32[2,1024]{1,0:T(2,128)} %owner_hbm.1) | copy-start | bytes 24580
  4.9 0.7 %copy-start.5 = (s32[8,8]{1,0:T(8,128)S(1)}, s32[8,8]{1,0:T(8,128)}, u32[]{:S(2)}) copy-start(s32[8,8]{1,0:T(8,128)} %lists_hbm.1) | copy-start | bytes 772
  5.5 0.7 %copy-start.6 = (f32[1024]{0:T(1024)S(1)}, f32[1024]{0:T(1024)}, u32[]{:S(2)}) copy-start(f32[1024]{0:T(1024)} %param.15) | copy-start | bytes 12292

commit v2 on v1

--- a/solution.py
+++ b/solution.py
@@ -1,4 +1,5 @@
 import functools
+import math
 
 import jax
 import jax.numpy as jnp
@@ -16,10 +17,12 @@
 WIDE = 2
 FAR = 3
 SPAN = 2 * FAR + 1
+WAITS = {0: (0, 1, -1), 2: (2, -2, 3, -3)}
 FORCE_SCALE = 0.02
 CORE_SQUARE = 0.25
 TIME_STEP = 4.0
 CENTRE = 2.0
+TOGETHER = 8
 F32 = jnp.float32
 BF16 = jnp.bfloat16
 MESH = pl.DeviceIdType.MESH
@@ -64,13 +67,18 @@
     list_own,
     list_far_v,
     list_far,
+    dense,
+    stage_f,
+    stage_p,
+    stage_q,
+    stage_a,
+    stage_n,
+    stage_t,
     feat,
-    tall,
-    feat_q,
-    feat_a,
     pull,
-    tgt_q,
-    tgt_a,
+    target,
+    goal,
+    codes_d,
     onehot,
     mask16,
     drag_send,
@@ -78,7 +86,6 @@
     eff,
     fbuf,
     vel,
-    mot,
     local_sem,
     send_a,
     recv_a,
@@ -159,64 +166,82 @@
             onehot[slot, :, span] = (rows == low).astype(F32).astype(BF16)
             rows16 = lax.broadcasted_iota(jnp.int32, (16, SEG), 0)
             mask16[slot, :, span] = (rows16 == high).astype(F32)
-
-    feat[...] = jnp.zeros_like(feat)
+            for b in range(NB):
+                codes_d[slot, e, b : b + 1, :] = node[:, b * BLK : (b + 1) * BLK]
+
+    ones = jnp.ones((NB, BLK), F32)
+    zeros = jnp.zeros((NB, BLK), F32)
+
+    def odd(rows):
+        return len(rows) | 1
+
+    def put(ref, base, rows):
+        for r, row in enumerate(rows):
+            ref[pl.ds(base * odd(rows) + r, NB, stride=odd(rows)), :] = row
+
+    def dense_fields(s):
+        for a, win in enumerate((win_c, win_l, win_b)):
+            for b in range(NB):
+                dense[s, pl.ds(24 * a + b, 3, stride=NB), :] = win[s, :, b * BLK : (b + 1) * BLK]
+        parts = [dense[s, NB * k : NB * (k + 1), :] for k in range(9)]
+        return [x - CENTRE for x in parts[0:3]], parts[3:6], parts[6:9]
+
+    def dot3(x, y):
+        return x[0] * y[0] + x[1] * y[1] + x[2] * y[2]
+
+    def split3(rows):
+        return [list(x) for x in zip(*(three_parts(row) for row in rows))]
+
+    def split2(rows):
+        return [list(x) for x in zip(*(two_parts(row) for row in rows))]
 
     def build_source(s):
-        c = win_c[s] - CENTRE
-        ch, cm, cl = three_parts(c)
-        for g, part in enumerate((ch, cm, ch, cm, cl, ch)):
-            feat[8 * g : 8 * g + 3, :] = part
-        rows = [win_c[s, k : k + 1, :] - CENTRE for k in range(3)]
-        square = rows[0] * rows[0] + rows[1] * rows[1] + rows[2] * rows[2] + CORE_SQUARE
-        for k, part in enumerate(three_parts(square)):
-            feat[48 + k : 49 + k, :] = part
-            feat[51 + k : 52 + k, :] = jnp.ones_like(part)
-        bh, bm, bl = three_parts(win_b[s])
-        for g, part in enumerate((bh, bm, bh, bm, bl, bh)):
-            feat[64 + 8 * g : 64 + 8 * g + 3, :] = part
-        line = [win_l[s, k : k + 1, :] for k in range(3)]
-        moment = (
-            line[1] * rows[2] - line[2] * rows[1],
-            line[2] * rows[0] - line[0] * rows[2],
-            line[0] * rows[1] - line[1] * rows[0],
+        c, line, burg = dense_fields(s)
+        ch, cm, cl = split3(c)
+        sh, sm, sl = three_parts(dot3(c, c) + CORE_SQUARE)
+        bh, bm = split2(burg)
+        rows = ch + cm + [sh, sm] + ch + cm + [ones, ones] + cl + ch + [sl, ones]
+        rows += (bh + bm + [zeros, zeros]) * 2 + [zeros] * 8
+        put(stage_f, s * NB, rows)
+        moment = [
+            line[1] * c[2] - line[2] * c[1],
+            line[2] * c[0] - line[0] * c[2],
+            line[0] * c[1] - line[1] * c[0],
+        ]
+        high, low = split2(line + moment)
+        put(stage_p, s * NB, high + [zeros, zeros] + low + [zeros, zeros])
+        for b in range(s * NB, (s + 1) * NB):
+            feat[b] = stage_f[49 * b : 49 * b + 48, :].astype(BF16)
+            pull[b] = stage_p[17 * b : 17 * b + 16, :].astype(BF16)
+        return c, line, (ch, cm, cl), (sh, sm)
+
+    centre_own, line_own, (ch, cm, cl), own_square = build_source(WIDE)
+
+    def twice(rows):
+        return [-2.0 * row for row in rows]
+
+    zh, zm, zl = three_parts(dot3(centre_own, centre_own))
+    lh, lm = split2(line_own)
+    rows = twice(ch) * 2 + [ones, ones] + twice(cm) * 2 + [zh, zm]
+    rows += twice(ch) + twice(cl) + [ones, zl]
+    put(stage_q, 0, rows)
+    put(stage_a, 0, lh * 2 + [zeros, zeros] + lm * 2 + [zeros, zeros])
+    for b in range(NB):
+        left = jnp.concatenate([stage_q[25 * b : 25 * b + 24, :], jnp.zeros((24, BLK), F32)], 0)
+        target[b, 0:BLK, :] = jnp.transpose(left).astype(BF16)
+        left = jnp.concatenate(
+            [
+                jnp.zeros((24, BLK), F32),
+                stage_a[17 * b : 17 * b + 16, :],
+                jnp.zeros((8, BLK), F32),
+            ],
+            0,
         )
-        for k in range(3):
-            lh, ll = two_parts(line[k])
-            mh, ml = two_parts(moment[k])
-            for g, part in enumerate((lh, mh, ll, ml)):
-                tall[8 * g + k : 8 * g + k + 1, :] = part
-        for b in range(NB):
-            cut = slice(b * BLK, (b + 1) * BLK)
-            feat_q[s * NB + b] = feat[0:64, cut].astype(BF16)
-            feat_a[s * NB + b] = feat[64:128, cut].astype(BF16)
-            pull[s * NB + b] = tall[:, cut].astype(BF16)
-            mot[s * NB + b, 0:3, :] = win_c[s, :, cut]
-
-    tall[...] = jnp.zeros_like(tall)
-    build_source(WIDE)
-
-    c = win_c[WIDE] - CENTRE
-    ch, cm, cl = three_parts(c)
-    for g, part in enumerate((ch, ch, cm, cm, ch, cl)):
-        feat[8 * g : 8 * g + 3, :] = -2.0 * part
-    rows = [win_c[WIDE, k : k + 1, :] - CENTRE for k in range(3)]
-    square = rows[0] * rows[0] + rows[1] * rows[1] + rows[2] * rows[2]
-    for k, part in enumerate(three_parts(square)):
-        feat[51 + k : 52 + k, :] = part
-        feat[48 + k : 49 + k, :] = jnp.ones_like(part)
-    lh, lm, ll = three_parts(win_l[WIDE])
-    for g, part in enumerate((lh, lh, lm, lm, lh, ll)):
-        feat[64 + 8 * g : 64 + 8 * g + 3, :] = part
-    for b in range(NB):
-        cut = slice(b * BLK, (b + 1) * BLK)
-        turned = jnp.transpose(feat[:, cut])
-        tgt_q[b] = turned[:, 0:64].astype(BF16)
-        tgt_a[b] = turned[:, 64:128].astype(BF16)
+        target[b, BLK : 2 * BLK, :] = jnp.transpose(left).astype(BF16)
 
     build_codes(FAR)
     line = [win_l[WIDE, k : k + 1, :] for k in range(3)]
-    length = 0.5 * jnp.sqrt(line[0] * line[0] + line[1] * line[1] + line[2] * line[2])
+    length = 0.5 * jnp.sqrt(dot3(line, line))
     drag = jnp.zeros((32, BLK), F32)
     for e in range(2):
         span = slice(e * SEG, (e + 1) * SEG)
@@ -235,10 +260,11 @@
     drag_copy.start()
     own_drag = drag[0:8] + drag[16:24]
 
+    kept_centres = {0: (centre_own, line_own, (ch, cm, cl), own_square)}
     for o in (1, -1, 2, -2):
         for a in range(3):
             sends_a[(-o, a)].wait_recv()
-        build_source(WIDE + o)
+        kept_centres[o] = build_source(WIDE + o)
     list_copy.wait_recv()
     to_smem = pltpu.make_async_copy(list_far_v, list_far, misc_sem.at[4])
     to_smem.start()
@@ -250,29 +276,29 @@
 
     def one_target(t, carry):
         block = HALF * lane + t
-        left_q = tgt_q[block]
-        left_a = tgt_a[block]
-        total = jnp.zeros((32, BLK), F32)
+        left = target[block]
+        total = jnp.zeros((16, BLK), F32)
         for lists in (list_own, list_far):
-            for e in range(NENT):
-                source = lists[block, e]
-                q = lax.dot_general(left_q, feat_q[source], NN, preferred_element_type=F32)
-                along = lax.dot_general(left_a, feat_a[source], NN, preferred_element_type=F32)
-                inverse = lax.rsqrt(q)
-                weight = along * inverse * inverse * inverse
+            for e in range(0, NENT, 2):
+                first = lists[block, e]
+                second = lists[block, e + 1]
+                right = jnp.concatenate([feat[first], feat[second]], axis=1)
+                both = lax.dot_general(left, right, NN, preferred_element_type=F32)
+                inverse = lax.rsqrt(both[0:BLK])
+                weight = both[BLK : 2 * BLK] * inverse * inverse * inverse
                 top = weight.astype(BF16)
                 low = (weight - top.astype(F32)).astype(BF16)
-                pulls = pull[source]
+                pulls = jnp.concatenate([pull[first], pull[second]], axis=1)
                 total = total + lax.dot_general(pulls, top, NT, preferred_element_type=F32)
                 total = total + lax.dot_general(pulls, low, NT, preferred_element_type=F32)
-        total = total[0:16] + total[16:32]
+        total = total[0:8] + total[8:16]
         cut = pl.ds(pl.multiple_of(block * BLK, BLK), BLK)
         x, y, z = (win_c[WIDE, k : k + 1, cut] - CENTRE for k in range(3))
         sx, sy, sz = (total[k : k + 1] for k in range(3))
         scale = 0.5 * FORCE_SCALE
-        fbuf[FAR, block, 0:1, :] = scale * (sy * z - sz * y - total[8:9])
-        fbuf[FAR, block, 1:2, :] = scale * (sz * x - sx * z - total[9:10])
-        fbuf[FAR, block, 2:3, :] = scale * (sx * y - sy * x - total[10:11])
+        fbuf[FAR, block, 0:1, :] = scale * (sy * z - sz * y - total[3:4])
+        fbuf[FAR, block, 1:2, :] = scale * (sz * x - sx * z - total[4:5])
+        fbuf[FAR, block, 2:3, :] = scale * (sx * y - sy * x - total[5:6])
         fbuf[FAR, block, 3:4, :] = eff[block]
         return carry
 
@@ -303,9 +329,10 @@
     recv_of = {(o, far): copy for (o, far), copy in zip(partners, sends_b)}
     for o in (0, 1, -1, 2, -2, 3, -3):
         slot = FAR + o
-        for far in (False, True):
-            if (-o, far) in recv_of:
-                recv_of[(-o, far)].wait_recv()
+        for group in WAITS.get(o, ()):
+            for far in (False, True):
+                if (-group, far) in recv_of:
+                    recv_of[(-group, far)].wait_recv()
         forces = jnp.concatenate([fbuf[slot, b] for b in range(NB)], axis=1)
         parts = two_parts(forces)
         total = jnp.zeros((96, BLK), F32)
@@ -336,49 +363,78 @@
                 for b in range(NB):
                     velocity_out[k : k + 1, b * BLK : (b + 1) * BLK] = value[b : b + 1, :]
 
-    for o in range(-WIDE, WIDE + 1):
+    shift = None
+    for o in (0, 1, -1, 2, -2):
         slot = FAR + o
-        table = jnp.concatenate(
-            [piece for k in range(3) for piece in (vel[slot, k], vel[slot + 1, k])], axis=0
-        )
-        stack = jnp.concatenate(two_parts(table), axis=0).astype(BF16)
-        both = None
+        s = WIDE + o
+        moved = [zeros, zeros, zeros]
         for e in range(2):
-            span = slice(e * SEG, (e + 1) * SEG)
-            picked = lax.dot_general(stack, onehot[slot, :, span], NN, preferred_element_type=F32)
-            picked = picked[0:48] + picked[48:96]
-            mask = mask16[slot, :, span] > 0.5
-            kept = [jnp.where(mask, picked[16 * k : 16 * k + 16], 0.0) for k in range(3)]
-            both = kept if both is None else [x + y for x, y in zip(both, kept)]
-        for k in range(3):
-            row = 0.5 * TIME_STEP * jnp.sum(both[k], axis=0, keepdims=True)
+            code = codes_d[slot, e]
+            low = jnp.bitwise_and(code, BLK - 1)
+            high = lax.shift_right_logical(code, 7)
+            picked = [zeros, zeros, zeros]
+            for h in range(16):
+                here = high == h
+                for k in range(3):
+                    row = vel[slot + h // NB, k, h % NB : h % NB + 1, :]
+                    table = jnp.broadcast_to(row, (NB, BLK))
+                    found = jnp.take_along_axis(table, low, axis=1, mode="promise_in_bounds")
+                    picked[k] = jnp.where(here, found, picked[k])
+            moved = [x + y for x, y in zip(moved, picked)]
+        moved = [0.5 * TIME_STEP * x for x in moved]
+        if shift is None:
+            shift = [
+                jnp.sum(jnp.sum(x, axis=1, keepdims=True), axis=0, keepdims=True) / SEG
+                for x in moved
+            ]
+        moved = [x - jnp.broadcast_to(y, (NB, BLK)) for x, y in zip(moved, shift)]
+        c, unused, (ch, cm, cl), (sh, sm) = kept_centres[o]
+        vh, vl = split2(moved)
+        ph, pm = two_parts(dot3(c, moved))
+        speed = dot3(moved, moved)
+        mh, ml = two_parts(speed + CORE_SQUARE)
+        rows = vh + vl + [ph, pm] + vh + vl + [ones, ones]
+        rows += ch + cm + [mh, ml] + ch + cm + [sh, sm]
+        put(stage_n, s * NB, rows)
+        if o == 0:
+            kh, kl = two_parts(speed)
+            zh, zm = two_parts(dot3(c, c))
+            none = [zeros, zeros]
+            rows = ch * 2 + [-ones, -ones] + cm * 2 + [-ph, -pm] + vh * 2 + none + vl * 2 + none
+            put(stage_t, 0, rows)
+            rows = twice(vh) * 2 + none + twice(vl) * 2 + [kh, kl]
+            rows += [zeros] * 6 + [ones, ones] + [zeros] * 8
+            put(stage_t, NB, rows)
+            rows = [zeros] * 14 + [zh, zm] + twice(ch) * 2 + none + twice(cm) * 2 + [ones, ones]
+            put(stage_t, 2 * NB, rows)
             for b in range(NB):
-                mot[(WIDE + o) * NB + b, 3 + k : 4 + k, :] = row[:, b * BLK : (b + 1) * BLK]
+                for g in range(3):
+                    rows_of = pl.ds(33 * (g * NB + b), 32)
+                    goal[b, :, g * BLK : (g + 1) * BLK] = stage_t[rows_of, :].astype(BF16)
 
     block_rows = lax.broadcasted_iota(jnp.int32, (NB, BLK), 0)
 
-    def one_pair(n, near):
-        target = cand_t[n]
-        source = cand_s[n]
-        here = mot[WIDE * NB + target]
-        there = jnp.transpose(mot[source])
-        goal = [jnp.broadcast_to(here[k : k + 1], (8, BLK)) for k in range(6)]
-        total = jnp.zeros((8, BLK), F32)
-        for r in range(BLK // 8):
-            chunk = there[8 * r : 8 * r + 8]
-            gap = [goal[k] - jnp.broadcast_to(chunk[:, k : k + 1], (8, BLK)) for k in range(6)]
-            x, y, z, u, v, w = gap
-            approach = x * u + y * v + z * w
-            square = u * u + v * v + w * w
-            fraction = jnp.clip(-approach / (square + CORE_SQUARE), 0.0, 1.0)
-            x = x + fraction * u
-            y = y + fraction * v
-            z = z + fraction * w
-            total = total + jnp.exp(-(x * x + y * y + z * z))
-        row = jnp.sum(total, axis=0, keepdims=True)
-        return near + jnp.where(block_rows == target, jnp.broadcast_to(row, (NB, BLK)), 0.0)
-
-    nearness_out[...] = lax.fori_loop(0, NCAND, one_pair, jnp.zeros((NB, BLK), F32))
+    def some_pairs(n, near):
+        for step in range(TOGETHER):
+            into = cand_t[TOGETHER * n + step]
+            source = cand_s[TOGETHER * n + step]
+            there = jnp.transpose(stage_n[pl.ds(source * 33, 32), :])
+            both = lax.dot_general(
+                there.astype(BF16), goal[into], NN, preferred_element_type=F32
+            )
+            ahead = both[:, 0:BLK]
+            square = both[:, BLK : 2 * BLK]
+            kept = jnp.minimum(jnp.maximum(ahead, 0.0), square)
+            fraction = kept / square
+            near_by = jnp.exp(
+                fraction * (2.0 * ahead - kept + CORE_SQUARE * fraction) - both[:, 2 * BLK :]
+            )
+            row = jnp.sum(near_by, axis=0, keepdims=True)
+            near = near + jnp.where(block_rows == into, jnp.broadcast_to(row, (NB, BLK)), 0.0)
+        return near
+
+    near = lax.fori_loop(0, NCAND // TOGETHER, some_pairs, jnp.zeros((NB, BLK), F32))
+    nearness_out[...] = math.exp(CORE_SQUARE) * near
 
     for copy in list(sends_a.values()) + list(sends_n.values()) + sends_b + [list_copy, drag_copy]:
         copy.wait_send()
@@ -418,13 +474,18 @@
             pltpu.SMEM((NB, NENT), jnp.int32),
             pltpu.VMEM((NB, NENT), jnp.int32),
             pltpu.SMEM((NB, NENT), jnp.int32),
-            pltpu.VMEM((128, SEG), F32),
-            pltpu.VMEM((32, SEG), F32),
-            pltpu.VMEM((window * NB, 64, BLK), BF16),
-            pltpu.VMEM((window * NB, 64, BLK), BF16),
-            pltpu.VMEM((window * NB, 32, BLK), BF16),
-            pltpu.VMEM((NB, BLK, 64), BF16),
-            pltpu.VMEM((NB, BLK, 64), BF16),
+            pltpu.VMEM((window, 72, BLK), F32),
+            pltpu.VMEM((window * NB * 49, BLK), F32),
+            pltpu.VMEM((window * NB * 17, BLK), F32),
+            pltpu.VMEM((NB * 25, BLK), F32),
+            pltpu.VMEM((NB * 17, BLK), F32),
+            pltpu.VMEM((window * NB * 33, BLK), F32),
+            pltpu.VMEM((3 * NB * 33, BLK), F32),
+            pltpu.VMEM((window * NB, 48, BLK), BF16),
+            pltpu.VMEM((window * NB, 16, BLK), BF16),
+            pltpu.VMEM((NB, 2 * BLK, 48), BF16),
+            pltpu.VMEM((NB, 32, 3 * BLK), BF16),
+            pltpu.VMEM((SPAN, 2, NB, BLK), jnp.int32),
             pltpu.VMEM((SPAN, BLK, 2 * SEG), BF16),
             pltpu.VMEM((SPAN, 16, 2 * SEG), F32),
             pltpu.VMEM((NB, BLK), F32),
@@ -432,7 +493,6 @@
             pltpu.VMEM((NB, 1, BLK), F32),
             pltpu.VMEM((SPAN, NB, 4, BLK), F32),
             pltpu.VMEM((SPAN, 3, NB, BLK), F32),
-            pltpu.VMEM((window * NB, 8, BLK), F32),
             pltpu.SemaphoreType.DMA((6,)),
             pltpu.SemaphoreType.DMA((window, 3)),
             pltpu.SemaphoreType.DMA((window, 3)),
@@ -443,7 +503,7 @@
             pltpu.SemaphoreType.DMA((SPAN, 2)),
         ],
         compiler_params=pltpu.CompilerParams(
-            collective_id=0, has_side_effects=True, vmem_limit_bytes=40 * 2**20
+            collective_id=0, has_side_effects=True, vmem_limit_bytes=60 * 1024 * 1024
         ),
     )(
         neighbour_blocks,

time: 53 us -> 35.2 us (0.66)
  Pallas kernels: 45 us -> 32.5 us
  local copies, waits for them, and re-layouts: 6.77 us -> 1.92 us
    pallas_call x1, Pallas kernels: 45 us -> 32.5 us  [local(): pl.pallas_call(functools.partial(kernel, n_cells), name='dislocation_step...]
    unnamed x20 -> x4, local copies, waits for them, and re-layouts: 6.77 us -> 1.92 us
where the time goes in v2:
time: 35.2 us; the launch traced here: 35 us
  Pallas kernels  32.5 us (92%)
  local copies, waits for them, and re-layouts  1.92 us (5%)
  between operations  0.65 us (2%)
    pallas_call x1, Pallas kernels, local(): pl.pallas_call(functools.partial(kernel, n_cells), name='dislocation_step...  32.5 us
    unnamed x4, local copies, waits for them, and re-layouts  1.92 us

profile of v2, /device:TPU:1, one launch (start us, length us, event | category | flops | bytes accessed | tf_op | source)
XLA Modules:
  0.0 35.0 jit_solution(12567611653450221419)
XLA Ops:
  0.6 32.5 %dislocation_step.1 = (f32[3,1024]{1,0:T(4,128)}, f32[8,128]{1,0:T(8,128)}) custom-call(s32[8,8]{1,0:T(8,128)} %lists_hbm.1, s32[32]{0:T(128)} %cand_t.1, s32[32]{0:T(128)} %cand_s.1, f32[3,1024]{1,0:T(4,128)} %centres_hbm.1, f32[3,1024]{1,0:T(4,128)} %lines_hbm.1, f32[3,1024]{1,0:T(4,128)} %burgers_hbm.1, s32[2,1024]{1,0:T(2,128)} %nodes_hbm.1, ...), custom_call_target="tpu_custom_call" | custom-call | tf_op jit(solution)/shard_map/dislocation_step/pallas_call | solution.py:459
  33.1 0.0 copy-start
  33.1 1.3 %copy.13 = f32[3,1024]{1,0:T(4,128)} copy(f32[3,1024]{1,0:T(4,128)} %get-tuple-element.8) | data formatting | bytes 24576
  34.4 0.0 copy-done
  34.4 0.6 %copy.14 = f32[1024]{0:T(1024)} copy(f32[1024]{0:T(1024)S(1)} %bitcast.3) | data formatting | bytes 8192
Async XLA Ops:
  33.1 1.3 %copy-start = (f32[8,128]{1,0:T(8,128)S(1)}, f32[8,128]{1,0:T(8,128)}, u32[]{:S(2)}) copy-start(f32[8,128]{1,0:T(8,128)} %get-tuple-element.5) | copy-start | bytes 12292

commit v3 on v2

--- a/solution.py
+++ b/solution.py
@@ -17,12 +17,12 @@
 WIDE = 2
 FAR = 3
 SPAN = 2 * FAR + 1
-WAITS = {0: (0, 1, -1), 2: (2, -2, 3, -3)}
 FORCE_SCALE = 0.02
 CORE_SQUARE = 0.25
 TIME_STEP = 4.0
 CENTRE = 2.0
 TOGETHER = 8
+AHEAD = 8
 F32 = jnp.float32
 BF16 = jnp.bfloat16
 MESH = pl.DeviceIdType.MESH
@@ -49,14 +49,14 @@
 def kernel(
     n_cells,
     lists_hbm,
-    cand_t,
-    cand_s,
+    cand_t_hbm,
+    cand_s_hbm,
     centres_hbm,
     lines_hbm,
     burgers_hbm,
     nodes_hbm,
     owner_hbm,
-    mobility,
+    mobility_hbm,
     velocity_out,
     nearness_out,
     win_c,
@@ -64,6 +64,9 @@
     win_b,
     codes_n,
     codes_o,
+    cand_t,
+    cand_s,
+    mobility,
     list_own,
     list_far_v,
     list_far,
@@ -106,8 +109,9 @@
         (o, far) for o in (0, 1, -1, 2, -2, 3, -3) for far in (False, True) if (o, far) != (0, False)
     ]
 
+    greeted = [(o, False) for o in (3, -3, 2, -2, 1, -1)] + [(0, True)]
     barrier = pltpu.get_barrier_semaphore()
-    for o, far in partners:
+    for o, far in greeted:
         pl.semaphore_signal(
             barrier, inc=1, device_id=(cell(o), other if far else lane), device_id_type=MESH
         )
@@ -118,10 +122,13 @@
         pltpu.make_async_copy(nodes_hbm, codes_n.at[FAR], local_sem.at[3]),
         pltpu.make_async_copy(owner_hbm, codes_o.at[FAR], local_sem.at[4]),
         pltpu.make_async_copy(lists_hbm, list_own, local_sem.at[5]),
+        pltpu.make_async_copy(mobility_hbm, mobility, local_sem.at[6]),
+        pltpu.make_async_copy(cand_t_hbm, cand_t, local_sem.at[7]),
+        pltpu.make_async_copy(cand_s_hbm, cand_s, local_sem.at[8]),
     ]
     for copy in own_copies:
         copy.start()
-    pl.semaphore_wait(barrier, len(partners))
+    pl.semaphore_wait(barrier, len(greeted))
 
     def remote(src, dst, send, recv, o, far):
         return pltpu.make_async_remote_copy(
@@ -211,8 +218,9 @@
         high, low = split2(line + moment)
         put(stage_p, s * NB, high + [zeros, zeros] + low + [zeros, zeros])
         for b in range(s * NB, (s + 1) * NB):
-            feat[b] = stage_f[49 * b : 49 * b + 48, :].astype(BF16)
-            pull[b] = stage_p[17 * b : 17 * b + 16, :].astype(BF16)
+            feat[b] = jnp.transpose(stage_f[49 * b : 49 * b + 48, :]).astype(BF16)
+            pulls = stage_p[17 * b : 17 * b + 16, :].astype(BF16)
+            pull[b] = jnp.concatenate([pulls, pulls], axis=1)
         return c, line, (ch, cm, cl), (sh, sm)
 
     centre_own, line_own, (ch, cm, cl), own_square = build_source(WIDE)
@@ -227,9 +235,9 @@
     put(stage_q, 0, rows)
     put(stage_a, 0, lh * 2 + [zeros, zeros] + lm * 2 + [zeros, zeros])
     for b in range(NB):
-        left = jnp.concatenate([stage_q[25 * b : 25 * b + 24, :], jnp.zeros((24, BLK), F32)], 0)
-        target[b, 0:BLK, :] = jnp.transpose(left).astype(BF16)
-        left = jnp.concatenate(
+        right = jnp.concatenate([stage_q[25 * b : 25 * b + 24, :], jnp.zeros((24, BLK), F32)], 0)
+        target[b, :, 0:BLK] = right.astype(BF16)
+        right = jnp.concatenate(
             [
                 jnp.zeros((24, BLK), F32),
                 stage_a[17 * b : 17 * b + 16, :],
@@ -237,7 +245,7 @@
             ],
             0,
         )
-        target[b, BLK : 2 * BLK, :] = jnp.transpose(left).astype(BF16)
+        target[b, :, BLK : 2 * BLK] = right.astype(BF16)
 
     build_codes(FAR)
     line = [win_l[WIDE, k : k + 1, :] for k in range(3)]
@@ -276,21 +284,28 @@
 
     def one_target(t, carry):
         block = HALF * lane + t
-        left = target[block]
+        right = target[block]
         total = jnp.zeros((16, BLK), F32)
-        for lists in (list_own, list_far):
-            for e in range(0, NENT, 2):
-                first = lists[block, e]
-                second = lists[block, e + 1]
-                right = jnp.concatenate([feat[first], feat[second]], axis=1)
-                both = lax.dot_general(left, right, NN, preferred_element_type=F32)
-                inverse = lax.rsqrt(both[0:BLK])
-                weight = both[BLK : 2 * BLK] * inverse * inverse * inverse
-                top = weight.astype(BF16)
-                low = (weight - top.astype(F32)).astype(BF16)
-                pulls = jnp.concatenate([pull[first], pull[second]], axis=1)
-                total = total + lax.dot_general(pulls, top, NT, preferred_element_type=F32)
-                total = total + lax.dot_general(pulls, low, NT, preferred_element_type=F32)
+        sources = [lists[block, e] for lists in (list_own, list_far) for e in range(NENT)]
+        ahead = []
+        for n in range(len(sources) + AHEAD):
+            if n < len(sources):
+                ahead.append(
+                    lax.dot_general(feat[sources[n]], right, NN, preferred_element_type=F32)
+                )
+            if n < AHEAD:
+                continue
+            both = ahead[n - AHEAD]
+            inverse = lax.rsqrt(both[:, 0:BLK])
+            weight = both[:, BLK : 2 * BLK] * inverse * inverse * inverse
+            top = weight.astype(BF16)
+            low = (weight - top.astype(F32)).astype(BF16)
+            total = total + lax.dot_general(
+                pull[sources[n - AHEAD]],
+                jnp.concatenate([top, low], axis=0),
+                NN,
+                preferred_element_type=F32,
+            )
         total = total[0:8] + total[8:16]
         cut = pl.ds(pl.multiple_of(block * BLK, BLK), BLK)
         x, y, z = (win_c[WIDE, k : k + 1, cut] - CENTRE for k in range(3))
@@ -303,6 +318,9 @@
         return carry
 
     lax.fori_loop(0, HALF, one_target, 0)
+
+    for copy in sends_n.values():
+        copy.wait_recv()
 
     mine = pl.ds(HALF * lane, HALF)
     sends_b = []
@@ -320,27 +338,32 @@
         sends_b.append(copy)
 
     for o in (1, -1, 2, -2, 3, -3):
-        for a in range(2):
-            sends_n[(-o, a)].wait_recv()
         build_codes(FAR + o)
+    for copy in list(sends_a.values()) + list(sends_n.values()) + [list_copy, drag_copy]:
+        copy.wait_send()
 
     own_part = {}
     next_part = {}
-    recv_of = {(o, far): copy for (o, far), copy in zip(partners, sends_b)}
-    for o in (0, 1, -1, 2, -2, 3, -3):
+    recv_of = dict(zip(partners, sends_b))
+
+    def wait_forces(o):
+        for far in (False, True):
+            if (-o, far) in recv_of:
+                recv_of[(-o, far)].wait_recv()
+
+    def scatter(o):
         slot = FAR + o
-        for group in WAITS.get(o, ()):
-            for far in (False, True):
-                if (-group, far) in recv_of:
-                    recv_of[(-group, far)].wait_recv()
         forces = jnp.concatenate([fbuf[slot, b] for b in range(NB)], axis=1)
         parts = two_parts(forces)
-        total = jnp.zeros((96, BLK), F32)
+        first = NB if o == -FAR else 0
+        last = NB if o == FAR else 2 * NB
+        size = last - first
+        total = jnp.zeros((6 * size, BLK), F32)
         for e in range(2):
             span = slice(e * SEG, (e + 1) * SEG)
-            mask = mask16[slot, :, span] > 0.5
+            mask = mask16[slot, first:last, span] > 0.5
             stack = [
-                jnp.where(mask, jnp.broadcast_to(part[k : k + 1], (16, SEG)), 0.0)
+                jnp.where(mask, jnp.broadcast_to(part[k : k + 1], (size, SEG)), 0.0)
                 for part in parts
                 for k in range(3)
             ]
@@ -350,11 +373,13 @@
                 NT,
                 preferred_element_type=F32,
             )
-        total = total[0:48] + total[48:96]
-        own_part[o] = [total[16 * k : 16 * k + 8] for k in range(3)]
-        next_part[o] = [total[16 * k + 8 : 16 * k + 16] for k in range(3)]
-
-    for o in range(-WIDE, FAR + 1):
+        total = total[0 : 3 * size] + total[3 * size : 6 * size]
+        if o < FAR:
+            next_part[o] = [total[size * (k + 1) - NB : size * (k + 1)] for k in range(3)]
+        if o > -FAR:
+            own_part[o] = [total[size * k : size * k + NB] for k in range(3)]
+
+    def node_velocity(o):
         eff_o = jnp.concatenate([fbuf[FAR + o, b, 3:4, :] for b in range(NB)], axis=0)
         for k in range(3):
             value = eff_o * (own_part[o][k] + next_part[o - 1][k])
@@ -363,8 +388,9 @@
                 for b in range(NB):
                     velocity_out[k : k + 1, b * BLK : (b + 1) * BLK] = value[b : b + 1, :]
 
-    shift = None
-    for o in (0, 1, -1, 2, -2):
+    shift = []
+
+    def gather(o):
         slot = FAR + o
         s = WIDE + o
         moved = [zeros, zeros, zeros]
@@ -382,11 +408,11 @@
                     picked[k] = jnp.where(here, found, picked[k])
             moved = [x + y for x, y in zip(moved, picked)]
         moved = [0.5 * TIME_STEP * x for x in moved]
-        if shift is None:
-            shift = [
+        if not shift:
+            shift.extend(
                 jnp.sum(jnp.sum(x, axis=1, keepdims=True), axis=0, keepdims=True) / SEG
                 for x in moved
-            ]
+            )
         moved = [x - jnp.broadcast_to(y, (NB, BLK)) for x, y in zip(moved, shift)]
         c, unused, (ch, cm, cl), (sh, sm) = kept_centres[o]
         vh, vl = split2(moved)
@@ -412,6 +438,23 @@
                     rows_of = pl.ds(33 * (g * NB + b), 32)
                     goal[b, :, g * BLK : (g + 1) * BLK] = stage_t[rows_of, :].astype(BF16)
 
+    for o in (0, 1, 2, 3):
+        wait_forces(o)
+    for o in (0, 1, 2, 3):
+        scatter(o)
+    for o in (1, 2, 3):
+        node_velocity(o)
+    for o in (1, 2):
+        gather(o)
+    for o in (-1, -2, -3):
+        wait_forces(o)
+    for o in (-1, -2, -3):
+        scatter(o)
+    for o in (0, -1, -2):
+        node_velocity(o)
+    for o in (0, -1, -2):
+        gather(o)
+
     block_rows = lax.broadcasted_iota(jnp.int32, (NB, BLK), 0)
 
     def some_pairs(n, near):
@@ -436,7 +479,7 @@
     near = lax.fori_loop(0, NCAND // TOGETHER, some_pairs, jnp.zeros((NB, BLK), F32))
     nearness_out[...] = math.exp(CORE_SQUARE) * near
 
-    for copy in list(sends_a.values()) + list(sends_n.values()) + sends_b + [list_copy, drag_copy]:
+    for copy in sends_b:
         copy.wait_send()
 
 
@@ -453,9 +496,8 @@
 ):
     n_cells = lax.axis_size("cells")
     window = 2 * WIDE + 1
-    anywhere = pl.BlockSpec(memory_space=pl.ANY)
+    hbm = pl.BlockSpec(memory_space=pltpu.HBM)
     vmem = pl.BlockSpec(memory_space=pltpu.VMEM)
-    smem = pl.BlockSpec(memory_space=pltpu.SMEM)
     velocity, nearness = pl.pallas_call(
         functools.partial(kernel, n_cells),
         name="dislocation_step",
@@ -463,7 +505,7 @@
             jax.ShapeDtypeStruct((3, SEG), F32),
             jax.ShapeDtypeStruct((NB, BLK), F32),
         ),
-        in_specs=[anywhere, smem, smem] + [anywhere] * 5 + [vmem],
+        in_specs=[hbm] * 9,
         out_specs=(vmem, vmem),
         scratch_shapes=[
             pltpu.VMEM((window, 3, SEG), F32),
@@ -471,6 +513,9 @@
             pltpu.VMEM((window, 3, SEG), F32),
             pltpu.VMEM((SPAN, 2, SEG), jnp.int32),
             pltpu.VMEM((SPAN, 2, SEG), jnp.int32),
+            pltpu.SMEM((NCAND,), jnp.int32),
+            pltpu.SMEM((NCAND,), jnp.int32),
+            pltpu.VMEM((NB, BLK), F32),
             pltpu.SMEM((NB, NENT), jnp.int32),
             pltpu.VMEM((NB, NENT), jnp.int32),
             pltpu.SMEM((NB, NENT), jnp.int32),
@@ -481,9 +526,9 @@
             pltpu.VMEM((NB * 17, BLK), F32),
             pltpu.VMEM((window * NB * 33, BLK), F32),
             pltpu.VMEM((3 * NB * 33, BLK), F32),
-            pltpu.VMEM((window * NB, 48, BLK), BF16),
-            pltpu.VMEM((window * NB, 16, BLK), BF16),
-            pltpu.VMEM((NB, 2 * BLK, 48), BF16),
+            pltpu.VMEM((window * NB, BLK, 48), BF16),
+            pltpu.VMEM((window * NB, 16, 2 * BLK), BF16),
+            pltpu.VMEM((NB, 48, 2 * BLK), BF16),
             pltpu.VMEM((NB, 32, 3 * BLK), BF16),
             pltpu.VMEM((SPAN, 2, NB, BLK), jnp.int32),
             pltpu.VMEM((SPAN, BLK, 2 * SEG), BF16),
@@ -493,7 +538,7 @@
             pltpu.VMEM((NB, 1, BLK), F32),
             pltpu.VMEM((SPAN, NB, 4, BLK), F32),
             pltpu.VMEM((SPAN, 3, NB, BLK), F32),
-            pltpu.SemaphoreType.DMA((6,)),
+            pltpu.SemaphoreType.DMA((9,)),
             pltpu.SemaphoreType.DMA((window, 3)),
             pltpu.SemaphoreType.DMA((window, 3)),
             pltpu.SemaphoreType.DMA((SPAN, 2)),

time: 35.2 us -> 33.5 us (0.952)
  Pallas kernels: 32.5 us -> 30.8 us
    pallas_call x1, Pallas kernels: 32.5 us -> 30.8 us  [local(): pl.pallas_call(functools.partial(kernel, n_cells), name='dislocation_step...]
where the time goes in v3:
time: 33.5 us; the launch traced here: 33.4 us
  Pallas kernels  30.8 us (92%)
  local copies, waits for them, and re-layouts  1.92 us (6%)
  between operations  0.65 us (2%)
    pallas_call x1, Pallas kernels, local(): pl.pallas_call(functools.partial(kernel, n_cells), name='dislocation_step...  30.8 us
    unnamed x4, local copies, waits for them, and re-layouts  1.92 us

profile of v3, /device:TPU:1, one launch (start us, length us, event | category | flops | bytes accessed | tf_op | source)
XLA Modules:
  0.0 33.4 jit_solution(17119178939602495447)
XLA Ops:
  0.6 30.8 %dislocation_step.1 = (f32[3,1024]{1,0:T(4,128)}, f32[8,128]{1,0:T(8,128)}) custom-call(s32[8,8]{1,0:T(8,128)} %lists_hbm.1, s32[32]{0:T(128)} %cand_t_hbm.1, s32[32]{0:T(128)} %cand_s_hbm.1, f32[3,1024]{1,0:T(4,128)} %centres_hbm.1, f32[3,1024]{1,0:T(4,128)} %lines_hbm.1, f32[3,1024]{1,0:T(4,128)} %burgers_hbm.1, s32[2,1024]{1,0:T(2,128)} %nodes_hbm.1, ...), custom_call_target="tpu_custom_call" | custom-call | tf_op jit(solution)/shard_map/dislocation_step/pallas_call | solution.py:501
  31.4 0.0 copy-start
  31.5 1.3 %copy.13 = f32[3,1024]{1,0:T(4,128)} copy(f32[3,1024]{1,0:T(4,128)} %get-tuple-element.8) | data formatting | bytes 24576
  32.8 0.0 copy-done
  32.8 0.6 %copy.14 = f32[1024]{0:T(1024)} copy(f32[1024]{0:T(1024)S(1)} %bitcast.3) | data formatting | bytes 8192
Async XLA Ops:
  31.4 1.3 %copy-start = (f32[8,128]{1,0:T(8,128)S(1)}, f32[8,128]{1,0:T(8,128)}, u32[]{:S(2)}) copy-start(f32[8,128]{1,0:T(8,128)} %get-tuple-element.5) | copy-start | bytes 12292

commit v4 on v3

--- a/solution.py
+++ b/solution.py
@@ -21,7 +21,8 @@
 CORE_SQUARE = 0.25
 TIME_STEP = 4.0
 CENTRE = 2.0
-TOGETHER = 8
+TOGETHER = 16
+SOONER = 4
 AHEAD = 8
 F32 = jnp.float32
 BF16 = jnp.bfloat16
@@ -62,8 +63,9 @@
     win_c,
     win_l,
     win_b,
-    codes_n,
-    codes_o,
+    nodes,
+    owner,
+    codes_r,
     cand_t,
     cand_s,
     mobility,
@@ -116,11 +118,11 @@
             barrier, inc=1, device_id=(cell(o), other if far else lane), device_id_type=MESH
         )
     own_copies = [
-        pltpu.make_async_copy(centres_hbm, win_c.at[WIDE], local_sem.at[0]),
-        pltpu.make_async_copy(lines_hbm, win_l.at[WIDE], local_sem.at[1]),
-        pltpu.make_async_copy(burgers_hbm, win_b.at[WIDE], local_sem.at[2]),
-        pltpu.make_async_copy(nodes_hbm, codes_n.at[FAR], local_sem.at[3]),
-        pltpu.make_async_copy(owner_hbm, codes_o.at[FAR], local_sem.at[4]),
+        pltpu.make_async_copy(centres_hbm, win_c, local_sem.at[0]),
+        pltpu.make_async_copy(lines_hbm, win_l, local_sem.at[1]),
+        pltpu.make_async_copy(burgers_hbm, win_b, local_sem.at[2]),
+        pltpu.make_async_copy(nodes_hbm, nodes, local_sem.at[3]),
+        pltpu.make_async_copy(owner_hbm, owner, local_sem.at[4]),
         pltpu.make_async_copy(lists_hbm, list_own, local_sem.at[5]),
         pltpu.make_async_copy(mobility_hbm, mobility, local_sem.at[6]),
         pltpu.make_async_copy(cand_t_hbm, cand_t, local_sem.at[7]),
@@ -128,6 +130,13 @@
     ]
     for copy in own_copies:
         copy.start()
+    for copy in own_copies:
+        copy.wait()
+
+    for a, win in enumerate((win_c, win_l, win_b)):
+        for b in range(NB):
+            dense[WIDE, pl.ds(24 * a + b, 3, stride=NB), :] = win[:, b * BLK : (b + 1) * BLK]
+    codes_r[FAR] = nodes[...] + SEG * owner[...]
     pl.semaphore_wait(barrier, len(greeted))
 
     def remote(src, dst, send, recv, o, far):
@@ -140,32 +149,26 @@
             device_id_type=MESH,
         )
 
-    sends_a = {}
-    for o in (1, -1, 2, -2):
-        for a, (src, dst) in enumerate(
-            ((centres_hbm, win_c), (lines_hbm, win_l), (burgers_hbm, win_b))
-        ):
-            slot = WIDE - o
-            sends_a[(o, a)] = remote(
-                src, dst.at[slot], send_a.at[WIDE + o, a], recv_a.at[slot, a], o, False
-            )
-            sends_a[(o, a)].start()
     list_copy = remote(lists_hbm, list_far_v, misc_sem.at[0], misc_sem.at[1], 0, True)
     list_copy.start()
+    sends_a = {}
+    for o in (-2, -1, 2, 1):
+        slot = WIDE - o
+        sends_a[o] = remote(
+            dense.at[WIDE], dense.at[slot], send_a.at[WIDE + o], recv_a.at[slot], o, False
+        )
+        sends_a[o].start()
     sends_n = {}
-    for o in (1, -1, 2, -2, 3, -3):
-        for a, (src, dst) in enumerate(((nodes_hbm, codes_n), (owner_hbm, codes_o))):
-            slot = FAR - o
-            sends_n[(o, a)] = remote(
-                src, dst.at[slot], send_n.at[FAR + o, a], recv_n.at[slot, a], o, False
-            )
-            sends_n[(o, a)].start()
-    for copy in own_copies:
-        copy.wait()
+    for o in (-3, -2, -1, 3, 2, 1):
+        slot = FAR - o
+        sends_n[o] = remote(
+            codes_r.at[FAR], codes_r.at[slot], send_n.at[FAR + o], recv_n.at[slot], o, False
+        )
+        sends_n[o].start()
 
     def build_codes(slot):
         for e in range(2):
-            node = codes_n[slot, e : e + 1, :] + SEG * codes_o[slot, e : e + 1, :]
+            node = codes_r[slot, e : e + 1, :]
             low = jnp.bitwise_and(node, BLK - 1)
             high = lax.shift_right_logical(node, 7)
             span = pl.ds(e * SEG, SEG)
@@ -187,9 +190,6 @@
             ref[pl.ds(base * odd(rows) + r, NB, stride=odd(rows)), :] = row
 
     def dense_fields(s):
-        for a, win in enumerate((win_c, win_l, win_b)):
-            for b in range(NB):
-                dense[s, pl.ds(24 * a + b, 3, stride=NB), :] = win[s, :, b * BLK : (b + 1) * BLK]
         parts = [dense[s, NB * k : NB * (k + 1), :] for k in range(9)]
         return [x - CENTRE for x in parts[0:3]], parts[3:6], parts[6:9]
 
@@ -248,7 +248,7 @@
         target[b, :, BLK : 2 * BLK] = right.astype(BF16)
 
     build_codes(FAR)
-    line = [win_l[WIDE, k : k + 1, :] for k in range(3)]
+    line = [win_l[k : k + 1, :] for k in range(3)]
     length = 0.5 * jnp.sqrt(dot3(line, line))
     drag = jnp.zeros((32, BLK), F32)
     for e in range(2):
@@ -270,8 +270,7 @@
 
     kept_centres = {0: (centre_own, line_own, (ch, cm, cl), own_square)}
     for o in (1, -1, 2, -2):
-        for a in range(3):
-            sends_a[(-o, a)].wait_recv()
+        sends_a[-o].wait_recv()
         kept_centres[o] = build_source(WIDE + o)
     list_copy.wait_recv()
     to_smem = pltpu.make_async_copy(list_far_v, list_far, misc_sem.at[4])
@@ -308,7 +307,7 @@
             )
         total = total[0:8] + total[8:16]
         cut = pl.ds(pl.multiple_of(block * BLK, BLK), BLK)
-        x, y, z = (win_c[WIDE, k : k + 1, cut] - CENTRE for k in range(3))
+        x, y, z = (win_c[k : k + 1, cut] - CENTRE for k in range(3))
         sx, sy, sz = (total[k : k + 1] for k in range(3))
         scale = 0.5 * FORCE_SCALE
         fbuf[FAR, block, 0:1, :] = scale * (sy * z - sz * y - total[3:4])
@@ -458,13 +457,16 @@
     block_rows = lax.broadcasted_iota(jnp.int32, (NB, BLK), 0)
 
     def some_pairs(n, near):
-        for step in range(TOGETHER):
-            into = cand_t[TOGETHER * n + step]
-            source = cand_s[TOGETHER * n + step]
-            there = jnp.transpose(stage_n[pl.ds(source * 33, 32), :])
-            both = lax.dot_general(
-                there.astype(BF16), goal[into], NN, preferred_element_type=F32
-            )
+        pairs = [(cand_t[TOGETHER * n + k], cand_s[TOGETHER * n + k]) for k in range(TOGETHER)]
+        dots = []
+        for k in range(TOGETHER + SOONER):
+            if k < TOGETHER:
+                into, source = pairs[k]
+                there = jnp.transpose(stage_n[pl.ds(source * 33, 32), :]).astype(BF16)
+                dots.append(lax.dot_general(there, goal[into], NN, preferred_element_type=F32))
+            if k < SOONER:
+                continue
+            into, both = pairs[k - SOONER][0], dots[k - SOONER]
             ahead = both[:, 0:BLK]
             square = both[:, BLK : 2 * BLK]
             kept = jnp.minimum(jnp.maximum(ahead, 0.0), square)
@@ -508,10 +510,11 @@
         in_specs=[hbm] * 9,
         out_specs=(vmem, vmem),
         scratch_shapes=[
-            pltpu.VMEM((window, 3, SEG), F32),
-            pltpu.VMEM((window, 3, SEG), F32),
-            pltpu.VMEM((window, 3, SEG), F32),
-            pltpu.VMEM((SPAN, 2, SEG), jnp.int32),
+            pltpu.VMEM((3, SEG), F32),
+            pltpu.VMEM((3, SEG), F32),
+            pltpu.VMEM((3, SEG), F32),
+            pltpu.VMEM((2, SEG), jnp.int32),
+            pltpu.VMEM((2, SEG), jnp.int32),
             pltpu.VMEM((SPAN, 2, SEG), jnp.int32),
             pltpu.SMEM((NCAND,), jnp.int32),
             pltpu.SMEM((NCAND,), jnp.int32),
@@ -539,10 +542,10 @@
             pltpu.VMEM((SPAN, NB, 4, BLK), F32),
             pltpu.VMEM((SPAN, 3, NB, BLK), F32),
             pltpu.SemaphoreType.DMA((9,)),
-            pltpu.SemaphoreType.DMA((window, 3)),
-            pltpu.SemaphoreType.DMA((window, 3)),
-            pltpu.SemaphoreType.DMA((SPAN, 2)),
-            pltpu.SemaphoreType.DMA((SPAN, 2)),
+            pltpu.SemaphoreType.DMA((window,)),
+            pltpu.SemaphoreType.DMA((window,)),
+            pltpu.SemaphoreType.DMA((SPAN,)),
+            pltpu.SemaphoreType.DMA((SPAN,)),
             pltpu.SemaphoreType.DMA((5,)),
             pltpu.SemaphoreType.DMA((SPAN, 2)),
             pltpu.SemaphoreType.DMA((SPAN, 2)),

time: 33.5 us -> 31.7 us (0.946)
  Pallas kernels: 30.8 us -> 29 us
    pallas_call x1, Pallas kernels: 30.8 us -> 29 us  [local(): pl.pallas_call(functools.partial(kernel, n_cells), name='dislocation_step...]
where the time goes in v4:
time: 31.7 us; the launch traced here: 31.5 us
  Pallas kernels  29 us (91%)
  local copies, waits for them, and re-layouts  1.92 us (6%)
  between operations  0.65 us (2%)
    pallas_call x1, Pallas kernels, local(): pl.pallas_call(functools.partial(kernel, n_cells), name='dislocation_step...  29 us
    unnamed x4, local copies, waits for them, and re-layouts  1.92 us

profile of v4, /device:TPU:1, one launch (start us, length us, event | category | flops | bytes accessed | tf_op | source)
XLA Modules:
  0.0 31.5 jit_solution(15780253892586759292)
XLA Ops:
  0.6 29.0 %dislocation_step.1 = (f32[3,1024]{1,0:T(4,128)}, f32[8,128]{1,0:T(8,128)}) custom-call(s32[8,8]{1,0:T(8,128)} %lists_hbm.1, s32[32]{0:T(128)} %cand_t_hbm.1, s32[32]{0:T(128)} %cand_s_hbm.1, f32[3,1024]{1,0:T(4,128)} %centres_hbm.1, f32[3,1024]{1,0:T(4,128)} %lines_hbm.1, f32[3,1024]{1,0:T(4,128)} %burgers_hbm.1, s32[2,1024]{1,0:T(2,128)} %nodes_hbm.1, ...), custom_call_target="tpu_custom_call" | custom-call | tf_op jit(solution)/shard_map/dislocation_step/pallas_call | solution.py:503
  29.6 0.0 copy-start
  29.6 1.3 %copy.13 = f32[3,1024]{1,0:T(4,128)} copy(f32[3,1024]{1,0:T(4,128)} %get-tuple-element.8) | data formatting | bytes 24576
  31.0 0.0 copy-done
  31.0 0.6 %copy.14 = f32[1024]{0:T(1024)} copy(f32[1024]{0:T(1024)S(1)} %bitcast.3) | data formatting | bytes 8192
Async XLA Ops:
  29.6 1.3 %copy-start = (f32[8,128]{1,0:T(8,128)S(1)}, f32[8,128]{1,0:T(8,128)}, u32[]{:S(2)}) copy-start(f32[8,128]{1,0:T(8,128)} %get-tuple-element.5) | copy-start | bytes 12292

commit v5 on v4

--- a/solution.py
+++ b/solution.py
@@ -24,10 +24,10 @@
 TOGETHER = 16
 SOONER = 4
 AHEAD = 8
+ABREAST = 4
 F32 = jnp.float32
 BF16 = jnp.bfloat16
 MESH = pl.DeviceIdType.MESH
-NT = (((1,), (1,)), ((), ()))
 NN = (((1,), (0,)), ((), ()))
 
 
@@ -108,7 +108,7 @@
         return lax.rem(me + (offset + n_cells), n_cells)
 
     partners = [
-        (o, far) for o in (0, 1, -1, 2, -2, 3, -3) for far in (False, True) if (o, far) != (0, False)
+        (o, far) for o in (3, -3, 2, -2, 1, -1, 0) for far in (True, False) if (o, far) != (0, False)
     ]
 
     greeted = [(o, False) for o in (3, -3, 2, -2, 1, -1)] + [(0, True)]
@@ -167,17 +167,20 @@
         sends_n[o].start()
 
     def build_codes(slot):
+        lanes = lax.broadcasted_iota(jnp.int32, (BLK, BLK), 1).astype(F32)
         for e in range(2):
             node = codes_r[slot, e : e + 1, :]
-            low = jnp.bitwise_and(node, BLK - 1)
             high = lax.shift_right_logical(node, 7)
-            span = pl.ds(e * SEG, SEG)
-            rows = lax.broadcasted_iota(jnp.int32, (BLK, SEG), 0)
-            onehot[slot, :, span] = (rows == low).astype(F32).astype(BF16)
             rows16 = lax.broadcasted_iota(jnp.int32, (16, SEG), 0)
-            mask16[slot, :, span] = (rows16 == high).astype(F32)
+            mask16[slot, :, pl.ds(e * SEG, SEG)] = (rows16 == high).astype(F32)
             for b in range(NB):
                 codes_d[slot, e, b : b + 1, :] = node[:, b * BLK : (b + 1) * BLK]
+            low = jnp.bitwise_and(codes_d[slot, e], BLK - 1).astype(F32)
+            turned = jnp.transpose(low)
+            for b in range(NB):
+                column = jnp.broadcast_to(turned[:, b : b + 1], (BLK, BLK))
+                rows = pl.ds(e * SEG + b * BLK, BLK)
+                onehot[slot, rows, :] = (column == lanes).astype(F32).astype(BF16)
 
     ones = jnp.ones((NB, BLK), F32)
     zeros = jnp.zeros((NB, BLK), F32)
@@ -259,8 +262,8 @@
         ]
         drag = drag + lax.dot_general(
             jnp.concatenate(parts, axis=0).astype(BF16),
-            onehot[FAR, :, span],
-            NT,
+            onehot[FAR, span, :],
+            NN,
             preferred_element_type=F32,
         )
     drag_send[...] = drag[8:16] + drag[24:32]
@@ -281,16 +284,22 @@
     for b in range(NB):
         eff[b] = eff_all[b : b + 1, :]
 
-    def one_target(t, carry):
-        block = HALF * lane + t
-        right = target[block]
-        total = jnp.zeros((16, BLK), F32)
-        sources = [lists[block, e] for lists in (list_own, list_far) for e in range(NENT)]
+    def some_targets(t, carry):
+        blocks = [HALF * lane + t * ABREAST + k for k in range(ABREAST)]
+        rights = [target[block] for block in blocks]
+        totals = [jnp.zeros((16, BLK), F32) for block in blocks]
+        sources = [
+            (k, lists[block, e])
+            for k, block in enumerate(blocks)
+            for lists in (list_own, list_far)
+            for e in range(NENT)
+        ]
         ahead = []
         for n in range(len(sources) + AHEAD):
             if n < len(sources):
+                k, source = sources[n]
                 ahead.append(
-                    lax.dot_general(feat[sources[n]], right, NN, preferred_element_type=F32)
+                    lax.dot_general(feat[source], rights[k], NN, preferred_element_type=F32)
                 )
             if n < AHEAD:
                 continue
@@ -299,24 +308,26 @@
             weight = both[:, BLK : 2 * BLK] * inverse * inverse * inverse
             top = weight.astype(BF16)
             low = (weight - top.astype(F32)).astype(BF16)
-            total = total + lax.dot_general(
-                pull[sources[n - AHEAD]],
+            k, source = sources[n - AHEAD]
+            totals[k] = totals[k] + lax.dot_general(
+                pull[source],
                 jnp.concatenate([top, low], axis=0),
                 NN,
                 preferred_element_type=F32,
             )
-        total = total[0:8] + total[8:16]
-        cut = pl.ds(pl.multiple_of(block * BLK, BLK), BLK)
-        x, y, z = (win_c[k : k + 1, cut] - CENTRE for k in range(3))
-        sx, sy, sz = (total[k : k + 1] for k in range(3))
-        scale = 0.5 * FORCE_SCALE
-        fbuf[FAR, block, 0:1, :] = scale * (sy * z - sz * y - total[3:4])
-        fbuf[FAR, block, 1:2, :] = scale * (sz * x - sx * z - total[4:5])
-        fbuf[FAR, block, 2:3, :] = scale * (sx * y - sy * x - total[5:6])
-        fbuf[FAR, block, 3:4, :] = eff[block]
+        for block, total in zip(blocks, totals):
+            total = total[0:8] + total[8:16]
+            cut = pl.ds(pl.multiple_of(block * BLK, BLK), BLK)
+            x, y, z = (win_c[k : k + 1, cut] - CENTRE for k in range(3))
+            sx, sy, sz = (total[k : k + 1] for k in range(3))
+            scale = 0.5 * FORCE_SCALE
+            fbuf[FAR, block, 0:1, :] = scale * (sy * z - sz * y - total[3:4])
+            fbuf[FAR, block, 1:2, :] = scale * (sz * x - sx * z - total[4:5])
+            fbuf[FAR, block, 2:3, :] = scale * (sx * y - sy * x - total[5:6])
+            fbuf[FAR, block, 3:4, :] = eff[block]
         return carry
 
-    lax.fori_loop(0, HALF, one_target, 0)
+    lax.fori_loop(0, HALF // ABREAST, some_targets, 0)
 
     for copy in sends_n.values():
         copy.wait_recv()
@@ -368,8 +379,8 @@
             ]
             total = total + lax.dot_general(
                 jnp.concatenate(stack, axis=0).astype(BF16),
-                onehot[slot, :, span],
-                NT,
+                onehot[slot, span, :],
+                NN,
                 preferred_element_type=F32,
             )
         total = total[0 : 3 * size] + total[3 * size : 6 * size]
@@ -504,8 +515,8 @@
         functools.partial(kernel, n_cells),
         name="dislocation_step",
         out_shape=(
-            jax.ShapeDtypeStruct((3, SEG), F32),
-            jax.ShapeDtypeStruct((NB, BLK), F32),
+            pltpu.VMEM((3, SEG), F32),
+            pltpu.VMEM((NB, BLK), F32),
         ),
         in_specs=[hbm] * 9,
         out_specs=(vmem, vmem),
@@ -534,7 +545,7 @@
             pltpu.VMEM((NB, 48, 2 * BLK), BF16),
             pltpu.VMEM((NB, 32, 3 * BLK), BF16),
             pltpu.VMEM((SPAN, 2, NB, BLK), jnp.int32),
-            pltpu.VMEM((SPAN, BLK, 2 * SEG), BF16),
+            pltpu.VMEM((SPAN, 2 * SEG, BLK), BF16),
             pltpu.VMEM((SPAN, 16, 2 * SEG), F32),
             pltpu.VMEM((NB, BLK), F32),
             pltpu.VMEM((NB, BLK), F32),

time: 31.7 us -> 28.8 us (0.909)
  Pallas kernels: 29 us -> 26.9 us
  local copies, waits for them, and re-layouts: 1.92 us -> 1.2 us
    pallas_call x1, Pallas kernels: 29 us -> 26.9 us  [local(): pl.pallas_call(functools.partial(kernel, n_cells), name='dislocation_step...]
    unnamed x4 -> x2, local copies, waits for them, and re-layouts: 1.92 us -> 1.2 us
where the time goes in v5:
time: 28.8 us; the launch traced here: 28.7 us
  Pallas kernels  26.9 us (93%)
  local copies, waits for them, and re-layouts  1.2 us (4%)
  between operations  0.64 us (2%)
    pallas_call x1, Pallas kernels, local(): pl.pallas_call(functools.partial(kernel, n_cells), name='dislocation_step...  26.9 us
    unnamed x2, local copies, waits for them, and re-layouts  1.2 us

profile of v5, /device:TPU:1, one launch (start us, length us, event | category | flops | bytes accessed | tf_op | source)
XLA Modules:
  0.0 28.7 jit_solution(13572719253656266980)
XLA Ops:
  0.6 26.9 %dislocation_step.1 = (f32[3,1024]{1,0:T(4,128)S(1)}, f32[8,128]{1,0:T(8,128)S(1)}) custom-call(s32[8,8]{1,0:T(8,128)} %lists_hbm.1, s32[32]{0:T(128)} %cand_t_hbm.1, s32[32]{0:T(128)} %cand_s_hbm.1, f32[3,1024]{1,0:T(4,128)} %centres_hbm.1, f32[3,1024]{1,0:T(4,128)} %lines_hbm.1, f32[3,1024]{1,0:T(4,128)} %burgers_hbm.1, s32[2,1024]{1,0:T(2,128)} %nodes_hbm.1, ...), custom_call_target="tpu_custom_call" | custom-call | tf_op jit(solution)/shard_map/dislocation_step/pallas_call | solution.py:514
  27.5 0.6 %copy.13 = f32[3,1024]{1,0:T(4,128)} copy(f32[3,1024]{1,0:T(4,128)S(1)} %get-tuple-element.6) | data formatting | bytes 24576
  28.1 0.6 %copy.14 = f32[1024]{0:T(1024)} copy(f32[1024]{0:T(1024)S(1)} %bitcast.2) | data formatting | bytes 8192

commit v6 on v5

--- a/solution.py
+++ b/solution.py
@@ -272,9 +272,14 @@
     own_drag = drag[0:8] + drag[16:24]
 
     kept_centres = {0: (centre_own, line_own, (ch, cm, cl), own_square)}
-    for o in (1, -1, 2, -2):
-        sends_a[-o].wait_recv()
-        kept_centres[o] = build_source(WIDE + o)
+
+    def sources_of(pair):
+        for o in pair:
+            sends_a[-o].wait_recv()
+        for o in pair:
+            kept_centres[o] = build_source(WIDE + o)
+
+    sources_of((-1, -2))
     list_copy.wait_recv()
     to_smem = pltpu.make_async_copy(list_far_v, list_far, misc_sem.at[4])
     to_smem.start()
@@ -283,6 +288,7 @@
     eff_all = mobility[...] / (1.0 + (own_drag + drag_recv[...]))
     for b in range(NB):
         eff[b] = eff_all[b : b + 1, :]
+    sources_of((1, 2))
 
     def some_targets(t, carry):
         blocks = [HALF * lane + t * ABREAST + k for k in range(ABREAST)]

time: 28.8 us -> 28.2 us (0.979)
  Pallas kernels: 26.9 us -> 26.2 us
    pallas_call x1, Pallas kernels: 26.9 us -> 26.2 us  [local(): pl.pallas_call(functools.partial(kernel, n_cells), name='dislocation_step...]
where the time goes in v6:
time: 28.2 us; the launch traced here: 28 us
  Pallas kernels  26.2 us (93%)
  local copies, waits for them, and re-layouts  1.2 us (4%)
  between operations  0.64 us (2%)
    pallas_call x1, Pallas kernels, local(): pl.pallas_call(functools.partial(kernel, n_cells), name='dislocation_step...  26.2 us
    unnamed x2, local copies, waits for them, and re-layouts  1.2 us

profile of v6, /device:TPU:1, one launch (start us, length us, event | category | flops | bytes accessed | tf_op | source)
XLA Modules:
  0.0 28.0 jit_solution(1325904394510046546)
XLA Ops:
  0.6 26.2 %dislocation_step.1 = (f32[3,1024]{1,0:T(4,128)S(1)}, f32[8,128]{1,0:T(8,128)S(1)}) custom-call(s32[8,8]{1,0:T(8,128)} %lists_hbm.1, s32[32]{0:T(128)} %cand_t_hbm.1, s32[32]{0:T(128)} %cand_s_hbm.1, f32[3,1024]{1,0:T(4,128)} %centres_hbm.1, f32[3,1024]{1,0:T(4,128)} %lines_hbm.1, f32[3,1024]{1,0:T(4,128)} %burgers_hbm.1, s32[2,1024]{1,0:T(2,128)} %nodes_hbm.1, ...), custom_call_target="tpu_custom_call" | custom-call | tf_op jit(solution)/shard_map/dislocation_step/pallas_call | solution.py:520
  26.8 0.6 %copy.13 = f32[3,1024]{1,0:T(4,128)} copy(f32[3,1024]{1,0:T(4,128)S(1)} %get-tuple-element.6) | data formatting | bytes 24576
  27.4 0.6 %copy.14 = f32[1024]{0:T(1024)} copy(f32[1024]{0:T(1024)S(1)} %bitcast.2) | data formatting | bytes 8192

commit v7 on v6

--- a/solution.py
+++ b/solution.py
@@ -405,6 +405,7 @@
                     velocity_out[k : k + 1, b * BLK : (b + 1) * BLK] = value[b : b + 1, :]
 
     shift = []
+    early = {}
 
     def gather(o):
         slot = FAR + o
@@ -414,8 +415,8 @@
             code = codes_d[slot, e]
             low = jnp.bitwise_and(code, BLK - 1)
             high = lax.shift_right_logical(code, 7)
-            picked = [zeros, zeros, zeros]
-            for h in range(16):
+            picked = early.get((o, e), [zeros, zeros, zeros])
+            for h in range(NB if (o, e) in early else 2 * NB):
                 here = high == h
                 for k in range(3):
                     row = vel[slot + h // NB, k, h % NB : h % NB + 1, :]
@@ -454,6 +455,20 @@
                     rows_of = pl.ds(33 * (g * NB + b), 32)
                     goal[b, :, g * BLK : (g + 1) * BLK] = stage_t[rows_of, :].astype(BF16)
 
+    def gather_early():
+        for e in range(2):
+            code = codes_d[FAR, e]
+            low = jnp.bitwise_and(code, BLK - 1)
+            high = lax.shift_right_logical(code, 7)
+            picked = [zeros, zeros, zeros]
+            for h in range(NB):
+                here = high == NB + h
+                for k in range(3):
+                    table = jnp.broadcast_to(vel[FAR + 1, k, h : h + 1, :], (NB, BLK))
+                    found = jnp.take_along_axis(table, low, axis=1, mode="promise_in_bounds")
+                    picked[k] = jnp.where(here, found, picked[k])
+            early[(0, e)] = picked
+
     for o in (0, 1, 2, 3):
         wait_forces(o)
     for o in (0, 1, 2, 3):
@@ -462,6 +477,7 @@
         node_velocity(o)
     for o in (1, 2):
         gather(o)
+    gather_early()
     for o in (-1, -2, -3):
         wait_forces(o)
     for o in (-1, -2, -3):

time: 28.2 us -> 28.2 us (level)
  no operation moved by 1% of the time
where the time goes in v7:
time: 28.2 us; the launch traced here: 28 us
  Pallas kernels  26.2 us (93%)
  local copies, waits for them, and re-layouts  1.2 us (4%)
  between operations  0.64 us (2%)
    pallas_call x1, Pallas kernels, local(): pl.pallas_call(functools.partial(kernel, n_cells), name='dislocation_step...  26.2 us
    unnamed x2, local copies, waits for them, and re-layouts  1.2 us

profile of v7, /device:TPU:1, one launch (start us, length us, event | category | flops | bytes accessed | tf_op | source)
XLA Modules:
  0.0 28.0 jit_solution(9111561423362517749)
XLA Ops:
  0.6 26.2 %dislocation_step.1 = (f32[3,1024]{1,0:T(4,128)S(1)}, f32[8,128]{1,0:T(8,128)S(1)}) custom-call(s32[8,8]{1,0:T(8,128)} %lists_hbm.1, s32[32]{0:T(128)} %cand_t_hbm.1, s32[32]{0:T(128)} %cand_s_hbm.1, f32[3,1024]{1,0:T(4,128)} %centres_hbm.1, f32[3,1024]{1,0:T(4,128)} %lines_hbm.1, f32[3,1024]{1,0:T(4,128)} %burgers_hbm.1, s32[2,1024]{1,0:T(2,128)} %nodes_hbm.1, ...), custom_call_target="tpu_custom_call" | custom-call | tf_op jit(solution)/shard_map/dislocation_step/pallas_call | solution.py:536
  26.8 0.6 %copy.13 = f32[3,1024]{1,0:T(4,128)} copy(f32[3,1024]{1,0:T(4,128)S(1)} %get-tuple-element.6) | data formatting | bytes 24576
  27.4 0.6 %copy.14 = f32[1024]{0:T(1024)} copy(f32[1024]{0:T(1024)S(1)} %bitcast.2) | data formatting | bytes 8192

commit v8 on v6

--- a/solution.py
+++ b/solution.py
@@ -288,7 +288,8 @@
     eff_all = mobility[...] / (1.0 + (own_drag + drag_recv[...]))
     for b in range(NB):
         eff[b] = eff_all[b : b + 1, :]
-    sources_of((1, 2))
+    sources_of((2,))
+    sources_of((1,))
 
     def some_targets(t, carry):
         blocks = [HALF * lane + t * ABREAST + k for k in range(ABREAST)]

time: 28.2 us -> 28.1 us (level)
  no operation moved by 1% of the time
where the time goes in v8:
time: 28.1 us; the launch traced here: 28 us
  Pallas kernels  26.1 us (93%)
  local copies, waits for them, and re-layouts  1.2 us (4%)
  between operations  0.64 us (2%)
    pallas_call x1, Pallas kernels, local(): pl.pallas_call(functools.partial(kernel, n_cells), name='dislocation_step...  26.1 us
    unnamed x2, local copies, waits for them, and re-layouts  1.2 us

profile of v8, /device:TPU:1, one launch (start us, length us, event | category | flops | bytes accessed | tf_op | source)
XLA Modules:
  0.0 28.0 jit_solution(14884558254697507729)
XLA Ops:
  0.6 26.1 %dislocation_step.1 = (f32[3,1024]{1,0:T(4,128)S(1)}, f32[8,128]{1,0:T(8,128)S(1)}) custom-call(s32[8,8]{1,0:T(8,128)} %lists_hbm.1, s32[32]{0:T(128)} %cand_t_hbm.1, s32[32]{0:T(128)} %cand_s_hbm.1, f32[3,1024]{1,0:T(4,128)} %centres_hbm.1, f32[3,1024]{1,0:T(4,128)} %lines_hbm.1, f32[3,1024]{1,0:T(4,128)} %burgers_hbm.1, s32[2,1024]{1,0:T(2,128)} %nodes_hbm.1, ...), custom_call_target="tpu_custom_call" | custom-call | tf_op jit(solution)/shard_map/dislocation_step/pallas_call | solution.py:521
  26.8 0.6 %copy.13 = f32[3,1024]{1,0:T(4,128)} copy(f32[3,1024]{1,0:T(4,128)S(1)} %get-tuple-element.6) | data formatting | bytes 24576
  27.4 0.6 %copy.14 = f32[1024]{0:T(1024)} copy(f32[1024]{0:T(1024)S(1)} %bitcast.2) | data formatting | bytes 8192
